TPU v7x, 256 devices: a whole 4x4x8 slice. The times are simulated.
256 devices in a mesh: slab: 64 (over z, y, core), quad: 4 (over x).
Axes of the slice: x: 4, y: 4, z: 8, core: 2. Of those that a mesh axis runs over, the one named last changes fastest.
Arguments:
- grain_cell: int32 [4, 2097152], P(None, ('slab', 'quad')), may hold values from 0 to 254, as said below
- grain_count: int32 [256], P(('slab', 'quad')), may hold values from 2048 to 8192, as said below
- grain_weight: float32 [2097152], P(('slab', 'quad')), may hold values from 0.05 to 0.95
- grain_volume: float32 [2097152], P(('slab', 'quad')), may hold values from 0.02 to 0.4
- grain_velocity: float32 [3, 2097152], P(None, ('slab', 'quad')), may hold values from -6 to 6
Outputs:
- pressure: float32 [256, 64, 256], P('slab', 'quad')
- drag: float32 [3, 2097152], P(None, ('slab', 'quad'))
Inputs may be any that keep to these rules, and one draw needn't show every extreme that they name: grain_cell[0] < 4, grain_cell[1] < 4, grain_cell[2] < 16, grain_cell[3] <= 254; among the slots of one device at most 4096 name the same quarter, and on every device exactly 4096 name one quarter. `grain_count`: some device has all 8192 slots occupied.
All inputs are finite; a program needn't handle non-finite values.
Results may differ from a plain program's by a relative error of at most 0.00002.
Values sent between devices are 32-bit elements; how exact they have to be, the bound alone decides.
A program may use at most 128 MiB of HBM per device.

v0:
```python
import jax
import jax.numpy as jnp
from jax import lax
from jax.sharding import PartitionSpec as P

CH = 4
CA = 16
CB = 256
ITERS = 12


damping = 0.05
source_gain = 4.0


def extended(block, sides, width):
    for axis, dim in sides:
        count = lax.axis_size(axis)
        forward = [(i, i + 1) for i in range(count - 1)]
        backward = [(target, source) for source, target in forward]
        low = lax.ppermute(
            lax.slice_in_dim(block, block.shape[dim] - width, None, axis=dim), axis, forward
        )
        high = lax.ppermute(lax.slice_in_dim(block, 0, width, axis=dim), axis, backward)
        block = jnp.concatenate([low, block, high], axis=dim)
    return block


def neighbours(padded):
    centre = padded[1:-1, 1:-1]
    along = jnp.pad(centre, ((0, 0), (0, 0), (1, 1)))
    total = padded[2:, 1:-1] + padded[:-2, 1:-1] + padded[1:-1, 2:] + padded[1:-1, :-2]
    return total + along[:, :, 2:] + along[:, :, :-2]


def gradient(wide):
    vel_height = -0.5 * (wide[2:, 1:-1, 1:-1] - wide[:-2, 1:-1, 1:-1])
    vel_across = -0.5 * (wide[1:-1, 2:, 1:-1] - wide[1:-1, :-2, 1:-1])
    vel_along = -0.5 * (wide[1:-1, 1:-1, 2:] - wide[1:-1, 1:-1, :-2])
    return (vel_height, vel_across, vel_along)


def body(grain_cell, grain_count, grain_weight, grain_volume, grain_velocity):
    quarters = lax.axis_size("quad")
    layers, across_cells, along_cells = (CH, CA, CB)
    block = layers * across_cells * along_cells
    slots = jnp.arange(grain_weight.shape[0], dtype=jnp.int32)
    valid = (slots < grain_count[0]).astype(jnp.float32)
    mass = valid * grain_volume
    upper = 1.0 - grain_weight
    target = (
        (grain_cell[0] * layers + grain_cell[1]) * across_cells + grain_cell[2]
    ) * along_cells + grain_cell[3]
    amounts = jnp.stack([mass, mass * grain_velocity[0]])
    partial_value = jnp.zeros((2, quarters * block), jnp.float32)
    partial_value = (
        partial_value.at[:, target]
        .add(amounts * grain_weight)
        .at[:, target + 1]
        .add(amounts * upper)
    )
    partial_value = partial_value.reshape(2, quarters * layers, across_cells, along_cells)
    field = lax.psum_scatter(partial_value, "quad", scatter_dimension=1, tiled=True)
    solid = field[0]
    voidage = 1.0 / (1.0 + solid)
    source = source_gain * field[1]
    start = jnp.zeros((layers, across_cells, along_cells), jnp.float32)

    def relax(repeat, pressure):
        padded = extended(pressure, (("slab", 0), ("quad", 1)), 1)
        return (source + voidage * neighbours(padded)) / (6.0 * voidage + damping)

    pressure = lax.fori_loop(0, ITERS, relax, start)
    rimmed_p = extended(pressure, (("slab", 0), ("quad", 1)), 1)
    vel_height, vel_across, vel_along = gradient(jnp.pad(rimmed_p, ((0, 0), (0, 0), (1, 1))))
    stacked = jnp.stack([vel_height, vel_across, vel_along, solid])
    table = lax.all_gather(stacked, "quad", axis=2, tiled=True)
    across_all = across_cells * quarters
    table = table.reshape(4, layers * across_all * along_cells)
    source_index = (
        grain_cell[1] * across_all + grain_cell[0] * across_cells + grain_cell[2]
    ) * along_cells + grain_cell[3]
    sampled = grain_weight * table[:, source_index] + upper * table[:, source_index + 1]
    factor = mass * (1.0 + sampled[3]) ** 2
    drag = factor * (sampled[:3] - grain_velocity)
    return (pressure, drag)


def solution(mesh):
    placed = (
        P(None, ("slab", "quad")),
        P(("slab", "quad")),
        P(("slab", "quad")),
        P(("slab", "quad")),
        P(None, ("slab", "quad")),
    )
    return jax.shard_map(
        body,
        mesh=mesh,
        in_specs=placed,
        out_specs=(P("slab", "quad", None), P(None, ("slab", "quad"))),
        check_vma=False,
    )
```

profile of v0, /device:TPU:121, one launch (start us, length us, event | category | flops | bytes accessed | tf_op | source)
XLA Modules:
  0.0 594.8 jit_solution(5532912857880428166)
XLA Ops:
  12.5 2.7 copy.19
  15.2 2.7 copy.20
  18.0 57.5 %scatter_custom_fusion = f32[2,65536]{0,1:T(8,128)} fusion(s32[8192]{0:T(1024)S(1)} %bitcast.61, f32[8192,2]{1,0:T(8,128)} %copy.19, f32[]{:T(128)} %constant.44.clone.1), kind=kCustom, calls=%fused_computation.26 | custom fusion | flops 16384 | bytes 524800 | tf_op jit(solution)/shard_map/scatter-add | solution.py:58
  75.5 61.4 %scatter_fusion = f32[2,65536]{0,1:T(8,128)} fusion(f32[2,65536]{0,1:T(8,128)} %scatter_custom_fusion, s32[8192]{0:T(1024)S(1)} %bitcast.58, f32[8192,2]{1,0:T(8,128)} %copy.20), kind=kCustom, calls=%fused_computation.3 | custom fusion | flops 16384 | bytes 229376 | tf_op jit(solution)/shard_map/scatter-add | solution.py:60
  136.9 20.1 %copy.21 = f32[2,16,16,256]{3,2,1,0:T(8,128)} copy(f32[2,16,16,256]{0,3,2,1:T(8,128)} %bitcast.51) | data formatting | bytes 1048576 | tf_op jit(solution)/shard_map/reshape | solution.py:62
  158.4 46.5 %all-reduce.5.cloned.1.call-done = f32[2,16,16,256]{3,2,1,0:T(8,128)} async-done(((f32[2,16,16,256]{3,2,1,0:T(8,128)}), f32[2,16,16,256]{3,2,1,0:T(8,128)}) %all-reduce.5.cloned.1.call-update) | async-done | bytes 524304
  205.8 216.4 %while.13 = (s32[]{:T(128)}, f32[4,16,256]{2,1,0:T(8,128)S(1)}, f32[4,16,256]{2,1,0:T(8,128)S(1)}, f32[4,16,256]{2,1,0:T(8,128)S(1)}, s32[]{:T(128)}, /*index=5*/s32[]{:T(128)}) while((s32[]{:T(128)}, f32[4,16,256]{2,1,0:T(8,128)S(1)}, f32[4,16,256]{2,1,0:T(8,128)S(1)}, f32[4,16,256]{2,1,0:T(8,128)S(1)}, s32[]{:T(128)}, ...), condition=%wide.region_4.5_spmd.clone, body=%wide.region_3.4_spmd.clone.sunk | while | flops 317443 | bytes 794863 | solution.py:73
  205.9 4.8 collective-permute-start
  210.7 4.2 collective-permute-start.1
  219.3 3.1 collective-permute-done.3
  222.5 3.2 collective-permute-start
  225.8 7.6 %collective-permute-start.1 = (f32[1,16,256]{2,1,0:T(8,128)S(1)}, f32[1,16,256]{2,1,0:T(8,128)S(1)}, u32[]{:S(2)}, u32[]{:S(2)}) collective-permute-start(f32[1,16,256]{2,1,0:T(8,128)S(1)} %get-tuple-element.140), channel_id=1, source_target_pairs={{0,4},{4,8},{8,12},{12,16},{16,20},{20,24},{24,28},{28,32},{32,36}... | collective-permute-start | bytes 49160 | tf_op jit(solution)/shard_map/while/body/eval_jaxpr/ppermute | solution.py:21
  234.2 3.4 collective-permute-start.2
  238.9 3.1 collective-permute-done.3
  244.1 9.0 %collective-permute-start.1 = (f32[1,16,256]{2,1,0:T(8,128)S(1)}, f32[1,16,256]{2,1,0:T(8,128)S(1)}, u32[]{:S(2)}, u32[]{:S(2)}) collective-permute-start(f32[1,16,256]{2,1,0:T(8,128)S(1)} %get-tuple-element.140), channel_id=1, source_target_pairs={{0,4},{4,8},{8,12},{12,16},{16,20},{20,24},{24,28},{28,32},{32,36}... | collective-permute-start | bytes 49160 | tf_op jit(solution)/shard_map/while/body/eval_jaxpr/ppermute | solution.py:21
  253.9 2.4 collective-permute-start.2
  257.7 3.1 collective-permute-done.3
  262.8 9.0 %collective-permute-start.1 = (f32[1,16,256]{2,1,0:T(8,128)S(1)}, f32[1,16,256]{2,1,0:T(8,128)S(1)}, u32[]{:S(2)}, u32[]{:S(2)}) collective-permute-start(f32[1,16,256]{2,1,0:T(8,128)S(1)} %get-tuple-element.140), channel_id=1, source_target_pairs={{0,4},{4,8},{8,12},{12,16},{16,20},{20,24},{24,28},{28,32},{32,36}... | collective-permute-start | bytes 49160 | tf_op jit(solution)/shard_map/while/body/eval_jaxpr/ppermute | solution.py:21
  275.6 3.1 collective-permute-done.3
  280.7 9.0 %collective-permute-start.1 = (f32[1,16,256]{2,1,0:T(8,128)S(1)}, f32[1,16,256]{2,1,0:T(8,128)S(1)}, u32[]{:S(2)}, u32[]{:S(2)}) collective-permute-start(f32[1,16,256]{2,1,0:T(8,128)S(1)} %get-tuple-element.140), channel_id=1, source_target_pairs={{0,4},{4,8},{8,12},{12,16},{16,20},{20,24},{24,28},{28,32},{32,36}... | collective-permute-start | bytes 49160 | tf_op jit(solution)/shard_map/while/body/eval_jaxpr/ppermute | solution.py:21
  293.5 3.1 collective-permute-done.3
  298.7 9.0 %collective-permute-start.1 = (f32[1,16,256]{2,1,0:T(8,128)S(1)}, f32[1,16,256]{2,1,0:T(8,128)S(1)}, u32[]{:S(2)}, u32[]{:S(2)}) collective-permute-start(f32[1,16,256]{2,1,0:T(8,128)S(1)} %get-tuple-element.140), channel_id=1, source_target_pairs={{0,4},{4,8},{8,12},{12,16},{16,20},{20,24},{24,28},{28,32},{32,36}... | collective-permute-start | bytes 49160 | tf_op jit(solution)/shard_map/while/body/eval_jaxpr/ppermute | solution.py:21
  311.5 3.1 collective-permute-done.3
  316.6 9.0 %collective-permute-start.1 = (f32[1,16,256]{2,1,0:T(8,128)S(1)}, f32[1,16,256]{2,1,0:T(8,128)S(1)}, u32[]{:S(2)}, u32[]{:S(2)}) collective-permute-start(f32[1,16,256]{2,1,0:T(8,128)S(1)} %get-tuple-element.140), channel_id=1, source_target_pairs={{0,4},{4,8},{8,12},{12,16},{16,20},{20,24},{24,28},{28,32},{32,36}... | collective-permute-start | bytes 49160 | tf_op jit(solution)/shard_map/while/body/eval_jaxpr/ppermute | solution.py:21
  329.4 3.1 collective-permute-done.3
  334.5 9.0 %collective-permute-start.1 = (f32[1,16,256]{2,1,0:T(8,128)S(1)}, f32[1,16,256]{2,1,0:T(8,128)S(1)}, u32[]{:S(2)}, u32[]{:S(2)}) collective-permute-start(f32[1,16,256]{2,1,0:T(8,128)S(1)} %get-tuple-element.140), channel_id=1, source_target_pairs={{0,4},{4,8},{8,12},{12,16},{16,20},{20,24},{24,28},{28,32},{32,36}... | collective-permute-start | bytes 49160 | tf_op jit(solution)/shard_map/while/body/eval_jaxpr/ppermute | solution.py:21
  347.3 3.1 collective-permute-done.3
  352.5 9.0 %collective-permute-start.1 = (f32[1,16,256]{2,1,0:T(8,128)S(1)}, f32[1,16,256]{2,1,0:T(8,128)S(1)}, u32[]{:S(2)}, u32[]{:S(2)}) collective-permute-start(f32[1,16,256]{2,1,0:T(8,128)S(1)} %get-tuple-element.140), channel_id=1, source_target_pairs={{0,4},{4,8},{8,12},{12,16},{16,20},{20,24},{24,28},{28,32},{32,36}... | collective-permute-start | bytes 49160 | tf_op jit(solution)/shard_map/while/body/eval_jaxpr/ppermute | solution.py:21
  365.2 3.1 collective-permute-done.3
  370.4 9.0 %collective-permute-start.1 = (f32[1,16,256]{2,1,0:T(8,128)S(1)}, f32[1,16,256]{2,1,0:T(8,128)S(1)}, u32[]{:S(2)}, u32[]{:S(2)}) collective-permute-start(f32[1,16,256]{2,1,0:T(8,128)S(1)} %get-tuple-element.140), channel_id=1, source_target_pairs={{0,4},{4,8},{8,12},{12,16},{16,20},{20,24},{24,28},{28,32},{32,36}... | collective-permute-start | bytes 49160 | tf_op jit(solution)/shard_map/while/body/eval_jaxpr/ppermute | solution.py:21
  383.2 3.1 collective-permute-done.3
  388.3 9.0 %collective-permute-start.1 = (f32[1,16,256]{2,1,0:T(8,128)S(1)}, f32[1,16,256]{2,1,0:T(8,128)S(1)}, u32[]{:S(2)}, u32[]{:S(2)}) collective-permute-start(f32[1,16,256]{2,1,0:T(8,128)S(1)} %get-tuple-element.140), channel_id=1, source_target_pairs={{0,4},{4,8},{8,12},{12,16},{16,20},{20,24},{24,28},{28,32},{32,36}... | collective-permute-start | bytes 49160 | tf_op jit(solution)/shard_map/while/body/eval_jaxpr/ppermute | solution.py:21
  401.1 3.1 collective-permute-done.3
  406.2 9.0 %collective-permute-start.1 = (f32[1,16,256]{2,1,0:T(8,128)S(1)}, f32[1,16,256]{2,1,0:T(8,128)S(1)}, u32[]{:S(2)}, u32[]{:S(2)}) collective-permute-start(f32[1,16,256]{2,1,0:T(8,128)S(1)} %get-tuple-element.140), channel_id=1, source_target_pairs={{0,4},{4,8},{8,12},{12,16},{16,20},{20,24},{24,28},{28,32},{32,36}... | collective-permute-start | bytes 49160 | tf_op jit(solution)/shard_map/while/body/eval_jaxpr/ppermute | solution.py:21
  419.0 3.1 collective-permute-done.3
  422.2 9.0 %collective-permute-start.5 = (f32[1,16,256]{2,1,0:T(8,128)S(1)}, f32[1,16,256]{2,1,0:T(8,128)S(1)}, u32[]{:S(2)}, u32[]{:S(2)}) collective-permute-start(f32[1,16,256]{2,1,0:T(8,128)S(1)} %get-tuple-element.105), channel_id=1, source_target_pairs={{0,4},{4,8},{8,12},{12,16},{16,20},{20,24},{24,28},{28,32},{32,36}... | collective-permute-start | bytes 49160 | tf_op jit(solution)/shard_map/ppermute | solution.py:21
  433.1 6.4 %collective-permute-done.4 = f32[1,16,256]{2,1,0:T(8,128)S(1)} collective-permute-done((f32[1,16,256]{2,1,0:T(8,128)S(1)}, f32[1,16,256]{2,1,0:T(8,128)S(1)}, u32[]{:S(2)}, u32[]{:S(2)}) %collective-permute-start.4) | collective-permute-done | bytes 16416 | tf_op jit(solution)/shard_map/ppermute | solution.py:24
  440.9 4.2 collective-permute-start.7
  446.8 22.3 %all-gather.2.cloned.1.call-done = f32[4,4,64,256]{3,2,1,0:T(8,128)} async-done(((f32[4,4,16,256]{3,2,1,0:T(8,128)}), f32[4,4,64,256]{3,2,1,0:T(8,128)}) %all-gather.2.cloned.1.call-update) | async-done | bytes 1048592 | tf_op jit(solution)/shard_map/all_gather | solution.py:77
  469.1 17.7 %copy.22 = f32[4,4,64,256]{0,3,2,1:T(8,128)} copy(f32[4,4,64,256]{3,2,1,0:T(8,128)} %all-gather.2.cloned.1.call-done) | data formatting | bytes 2097152 | tf_op jit(solution)/shard_map/all_gather | solution.py:77
  486.8 38.4 %gather_fusion = f32[8192,4]{1,0:T(8,128)} fusion(f32[4,65536]{0,1:T(8,128)} %bitcast.52, s32[8192]{0:T(1024)S(1)} %broadcast_clamp_fusion.1), kind=kCustom, calls=%fused_computation | custom fusion | bytes 294912 | tf_op jit(solution)/shard_map/gather | solution.py:83
  525.2 38.4 %gather_fusion.1 = f32[8192,4]{1,0:T(8,128)} fusion(f32[4,65536]{0,1:T(8,128)} %bitcast.53, s32[8192]{0:T(1024)S(1)} %broadcast_clamp_fusion), kind=kCustom, calls=%fused_computation.1 | custom fusion | bytes 294912 | tf_op jit(solution)/shard_map/gather | solution.py:83
  563.6 7.0 %add_bitcast_fusion = f32[4,8192]{0,1:T(8,128)S(1)} fusion(f32[8192,4]{1,0:T(8,128)} %gather_fusion.1, f32[8192,4]{1,0:T(8,128)} %gather_fusion, f32[8192]{0:T(1024)S(1)} %broadcast_subtract_fusion, f32[8192]{0:T(1024)S(1)} %copy-done.2), kind=kLoop, calls=%fused_computation.31 | loop fusion | flops 98304 | bytes 458752 | tf_op jit(solution)/shard_map/add | solution.py:83
  572.6 2.2 fusion.11
  574.8 2.8 copy.23
  577.7 2.6 copy.24
  580.4 4.2 broadcast_multiply_fusion
  584.5 3.5 copy.25
  (157 shorter events, 76.5 us)
Async XLA Ops:
  7.2 197.8 %all-reduce.5.cloned.1.call-start = ((), (), s32[]{:S(2)}) async-start(), calls=%async_computation.1 | async-start | bytes 1048576
  157.1 311.9 %all-gather.2.cloned.1.call-start = ((), (), s32[]{:S(2)}) async-start(), calls=%async_computation | async-start | bytes 1310720 | tf_op jit(solution)/shard_map/all_gather | solution.py:77
  205.9 9.0 %collective-permute-start = (f32[1,16,256]{2,1,0:T(8,128)S(1)}, f32[1,16,256]{2,1,0:T(8,128)S(1)}, u32[]{:S(2)}, u32[]{:S(2)}) collective-permute-start(f32[1,16,256]{2,1,0:T(8,128)S(1)} %get-tuple-element.139), channel_id=1, source_target_pairs={{4,0},{8,4},{12,8},{16,12},{20,16},{24,20},{28,24},{32,28},{36,32}... | collective-permute-start | bytes 49160 | tf_op jit(solution)/shard_map/while/body/eval_jaxpr/ppermute | solution.py:24
  210.7 5.1 collective-permute-start.1
  215.8 3.5 collective-permute-start.2
  217.9 4.4 collective-permute-start.3
  222.5 10.9 %collective-permute-start = (f32[1,16,256]{2,1,0:T(8,128)S(1)}, f32[1,16,256]{2,1,0:T(8,128)S(1)}, u32[]{:S(2)}, u32[]{:S(2)}) collective-permute-start(f32[1,16,256]{2,1,0:T(8,128)S(1)} %get-tuple-element.139), channel_id=1, source_target_pairs={{4,0},{8,4},{12,8},{16,12},{20,16},{24,20},{28,24},{32,28},{36,32}... | collective-permute-start | bytes 49160 | tf_op jit(solution)/shard_map/while/body/eval_jaxpr/ppermute | solution.py:24
  225.8 8.5 %collective-permute-start.1 = (f32[1,16,256]{2,1,0:T(8,128)S(1)}, f32[1,16,256]{2,1,0:T(8,128)S(1)}, u32[]{:S(2)}, u32[]{:S(2)}) collective-permute-start(f32[1,16,256]{2,1,0:T(8,128)S(1)} %get-tuple-element.140), channel_id=1, source_target_pairs={{0,4},{4,8},{8,12},{12,16},{16,20},{20,24},{24,28},{28,32},{32,36}... | collective-permute-start | bytes 49160 | tf_op jit(solution)/shard_map/while/body/eval_jaxpr/ppermute | solution.py:21
  234.2 4.7 collective-permute-start.2
  237.6 4.4 collective-permute-start.3
  242.2 10.9 %collective-permute-start = (f32[1,16,256]{2,1,0:T(8,128)S(1)}, f32[1,16,256]{2,1,0:T(8,128)S(1)}, u32[]{:S(2)}, u32[]{:S(2)}) collective-permute-start(f32[1,16,256]{2,1,0:T(8,128)S(1)} %get-tuple-element.139), channel_id=1, source_target_pairs={{4,0},{8,4},{12,8},{16,12},{20,16},{24,20},{28,24},{32,28},{36,32}... | collective-permute-start | bytes 49160 | tf_op jit(solution)/shard_map/while/body/eval_jaxpr/ppermute | solution.py:24
  244.1 9.8 %collective-permute-start.1 = (f32[1,16,256]{2,1,0:T(8,128)S(1)}, f32[1,16,256]{2,1,0:T(8,128)S(1)}, u32[]{:S(2)}, u32[]{:S(2)}) collective-permute-start(f32[1,16,256]{2,1,0:T(8,128)S(1)} %get-tuple-element.140), channel_id=1, source_target_pairs={{0,4},{4,8},{8,12},{12,16},{16,20},{20,24},{24,28},{28,32},{32,36}... | collective-permute-start | bytes 49160 | tf_op jit(solution)/shard_map/while/body/eval_jaxpr/ppermute | solution.py:21
  253.9 3.8 collective-permute-start.2
  256.4 4.4 collective-permute-start.3
  260.9 10.9 %collective-permute-start = (f32[1,16,256]{2,1,0:T(8,128)S(1)}, f32[1,16,256]{2,1,0:T(8,128)S(1)}, u32[]{:S(2)}, u32[]{:S(2)}) collective-permute-start(f32[1,16,256]{2,1,0:T(8,128)S(1)} %get-tuple-element.139), channel_id=1, source_target_pairs={{4,0},{8,4},{12,8},{16,12},{20,16},{24,20},{28,24},{32,28},{36,32}... | collective-permute-start | bytes 49160 | tf_op jit(solution)/shard_map/while/body/eval_jaxpr/ppermute | solution.py:24
  262.8 9.8 %collective-permute-start.1 = (f32[1,16,256]{2,1,0:T(8,128)S(1)}, f32[1,16,256]{2,1,0:T(8,128)S(1)}, u32[]{:S(2)}, u32[]{:S(2)}) collective-permute-start(f32[1,16,256]{2,1,0:T(8,128)S(1)} %get-tuple-element.140), channel_id=1, source_target_pairs={{0,4},{4,8},{8,12},{12,16},{16,20},{20,24},{24,28},{28,32},{32,36}... | collective-permute-start | bytes 49160 | tf_op jit(solution)/shard_map/while/body/eval_jaxpr/ppermute | solution.py:21
  274.3 4.4 collective-permute-start.3
  278.8 10.9 %collective-permute-start = (f32[1,16,256]{2,1,0:T(8,128)S(1)}, f32[1,16,256]{2,1,0:T(8,128)S(1)}, u32[]{:S(2)}, u32[]{:S(2)}) collective-permute-start(f32[1,16,256]{2,1,0:T(8,128)S(1)} %get-tuple-element.139), channel_id=1, source_target_pairs={{4,0},{8,4},{12,8},{16,12},{20,16},{24,20},{28,24},{32,28},{36,32}... | collective-permute-start | bytes 49160 | tf_op jit(solution)/shard_map/while/body/eval_jaxpr/ppermute | solution.py:24
  280.7 9.8 %collective-permute-start.1 = (f32[1,16,256]{2,1,0:T(8,128)S(1)}, f32[1,16,256]{2,1,0:T(8,128)S(1)}, u32[]{:S(2)}, u32[]{:S(2)}) collective-permute-start(f32[1,16,256]{2,1,0:T(8,128)S(1)} %get-tuple-element.140), channel_id=1, source_target_pairs={{0,4},{4,8},{8,12},{12,16},{16,20},{20,24},{24,28},{28,32},{32,36}... | collective-permute-start | bytes 49160 | tf_op jit(solution)/shard_map/while/body/eval_jaxpr/ppermute | solution.py:21
  290.6 3.0 collective-permute-start.2
  292.2 4.4 collective-permute-start.3
  296.7 10.9 %collective-permute-start = (f32[1,16,256]{2,1,0:T(8,128)S(1)}, f32[1,16,256]{2,1,0:T(8,128)S(1)}, u32[]{:S(2)}, u32[]{:S(2)}) collective-permute-start(f32[1,16,256]{2,1,0:T(8,128)S(1)} %get-tuple-element.139), channel_id=1, source_target_pairs={{4,0},{8,4},{12,8},{16,12},{20,16},{24,20},{28,24},{32,28},{36,32}... | collective-permute-start | bytes 49160 | tf_op jit(solution)/shard_map/while/body/eval_jaxpr/ppermute | solution.py:24
  298.7 9.8 %collective-permute-start.1 = (f32[1,16,256]{2,1,0:T(8,128)S(1)}, f32[1,16,256]{2,1,0:T(8,128)S(1)}, u32[]{:S(2)}, u32[]{:S(2)}) collective-permute-start(f32[1,16,256]{2,1,0:T(8,128)S(1)} %get-tuple-element.140), channel_id=1, source_target_pairs={{0,4},{4,8},{8,12},{12,16},{16,20},{20,24},{24,28},{28,32},{32,36}... | collective-permute-start | bytes 49160 | tf_op jit(solution)/shard_map/while/body/eval_jaxpr/ppermute | solution.py:21
  308.5 3.0 collective-permute-start.2
  310.1 4.4 collective-permute-start.3
  314.7 10.9 %collective-permute-start = (f32[1,16,256]{2,1,0:T(8,128)S(1)}, f32[1,16,256]{2,1,0:T(8,128)S(1)}, u32[]{:S(2)}, u32[]{:S(2)}) collective-permute-start(f32[1,16,256]{2,1,0:T(8,128)S(1)} %get-tuple-element.139), channel_id=1, source_target_pairs={{4,0},{8,4},{12,8},{16,12},{20,16},{24,20},{28,24},{32,28},{36,32}... | collective-permute-start | bytes 49160 | tf_op jit(solution)/shard_map/while/body/eval_jaxpr/ppermute | solution.py:24
  316.6 9.8 %collective-permute-start.1 = (f32[1,16,256]{2,1,0:T(8,128)S(1)}, f32[1,16,256]{2,1,0:T(8,128)S(1)}, u32[]{:S(2)}, u32[]{:S(2)}) collective-permute-start(f32[1,16,256]{2,1,0:T(8,128)S(1)} %get-tuple-element.140), channel_id=1, source_target_pairs={{0,4},{4,8},{8,12},{12,16},{16,20},{20,24},{24,28},{28,32},{32,36}... | collective-permute-start | bytes 49160 | tf_op jit(solution)/shard_map/while/body/eval_jaxpr/ppermute | solution.py:21
  328.1 4.4 collective-permute-start.3
  332.6 10.9 %collective-permute-start = (f32[1,16,256]{2,1,0:T(8,128)S(1)}, f32[1,16,256]{2,1,0:T(8,128)S(1)}, u32[]{:S(2)}, u32[]{:S(2)}) collective-permute-start(f32[1,16,256]{2,1,0:T(8,128)S(1)} %get-tuple-element.139), channel_id=1, source_target_pairs={{4,0},{8,4},{12,8},{16,12},{20,16},{24,20},{28,24},{32,28},{36,32}... | collective-permute-start | bytes 49160 | tf_op jit(solution)/shard_map/while/body/eval_jaxpr/ppermute | solution.py:24
  334.5 9.8 %collective-permute-start.1 = (f32[1,16,256]{2,1,0:T(8,128)S(1)}, f32[1,16,256]{2,1,0:T(8,128)S(1)}, u32[]{:S(2)}, u32[]{:S(2)}) collective-permute-start(f32[1,16,256]{2,1,0:T(8,128)S(1)} %get-tuple-element.140), channel_id=1, source_target_pairs={{0,4},{4,8},{8,12},{12,16},{16,20},{20,24},{24,28},{28,32},{32,36}... | collective-permute-start | bytes 49160 | tf_op jit(solution)/shard_map/while/body/eval_jaxpr/ppermute | solution.py:21
  344.3 3.0 collective-permute-start.2
  346.0 4.4 collective-permute-start.3
  350.5 10.9 %collective-permute-start = (f32[1,16,256]{2,1,0:T(8,128)S(1)}, f32[1,16,256]{2,1,0:T(8,128)S(1)}, u32[]{:S(2)}, u32[]{:S(2)}) collective-permute-start(f32[1,16,256]{2,1,0:T(8,128)S(1)} %get-tuple-element.139), channel_id=1, source_target_pairs={{4,0},{8,4},{12,8},{16,12},{20,16},{24,20},{28,24},{32,28},{36,32}... | collective-permute-start | bytes 49160 | tf_op jit(solution)/shard_map/while/body/eval_jaxpr/ppermute | solution.py:24
  352.5 9.8 %collective-permute-start.1 = (f32[1,16,256]{2,1,0:T(8,128)S(1)}, f32[1,16,256]{2,1,0:T(8,128)S(1)}, u32[]{:S(2)}, u32[]{:S(2)}) collective-permute-start(f32[1,16,256]{2,1,0:T(8,128)S(1)} %get-tuple-element.140), channel_id=1, source_target_pairs={{0,4},{4,8},{8,12},{12,16},{16,20},{20,24},{24,28},{28,32},{32,36}... | collective-permute-start | bytes 49160 | tf_op jit(solution)/shard_map/while/body/eval_jaxpr/ppermute | solution.py:21
  363.9 4.4 collective-permute-start.3
  368.5 10.9 %collective-permute-start = (f32[1,16,256]{2,1,0:T(8,128)S(1)}, f32[1,16,256]{2,1,0:T(8,128)S(1)}, u32[]{:S(2)}, u32[]{:S(2)}) collective-permute-start(f32[1,16,256]{2,1,0:T(8,128)S(1)} %get-tuple-element.139), channel_id=1, source_target_pairs={{4,0},{8,4},{12,8},{16,12},{20,16},{24,20},{28,24},{32,28},{36,32}... | collective-permute-start | bytes 49160 | tf_op jit(solution)/shard_map/while/body/eval_jaxpr/ppermute | solution.py:24
  370.4 9.8 %collective-permute-start.1 = (f32[1,16,256]{2,1,0:T(8,128)S(1)}, f32[1,16,256]{2,1,0:T(8,128)S(1)}, u32[]{:S(2)}, u32[]{:S(2)}) collective-permute-start(f32[1,16,256]{2,1,0:T(8,128)S(1)} %get-tuple-element.140), channel_id=1, source_target_pairs={{0,4},{4,8},{8,12},{12,16},{16,20},{20,24},{24,28},{28,32},{32,36}... | collective-permute-start | bytes 49160 | tf_op jit(solution)/shard_map/while/body/eval_jaxpr/ppermute | solution.py:21
  381.9 4.4 collective-permute-start.3
  386.4 10.9 %collective-permute-start = (f32[1,16,256]{2,1,0:T(8,128)S(1)}, f32[1,16,256]{2,1,0:T(8,128)S(1)}, u32[]{:S(2)}, u32[]{:S(2)}) collective-permute-start(f32[1,16,256]{2,1,0:T(8,128)S(1)} %get-tuple-element.139), channel_id=1, source_target_pairs={{4,0},{8,4},{12,8},{16,12},{20,16},{24,20},{28,24},{32,28},{36,32}... | collective-permute-start | bytes 49160 | tf_op jit(solution)/shard_map/while/body/eval_jaxpr/ppermute | solution.py:24
  388.3 9.8 %collective-permute-start.1 = (f32[1,16,256]{2,1,0:T(8,128)S(1)}, f32[1,16,256]{2,1,0:T(8,128)S(1)}, u32[]{:S(2)}, u32[]{:S(2)}) collective-permute-start(f32[1,16,256]{2,1,0:T(8,128)S(1)} %get-tuple-element.140), channel_id=1, source_target_pairs={{0,4},{4,8},{8,12},{12,16},{16,20},{20,24},{24,28},{28,32},{32,36}... | collective-permute-start | bytes 49160 | tf_op jit(solution)/shard_map/while/body/eval_jaxpr/ppermute | solution.py:21
  399.8 4.4 collective-permute-start.3
  404.3 10.9 %collective-permute-start = (f32[1,16,256]{2,1,0:T(8,128)S(1)}, f32[1,16,256]{2,1,0:T(8,128)S(1)}, u32[]{:S(2)}, u32[]{:S(2)}) collective-permute-start(f32[1,16,256]{2,1,0:T(8,128)S(1)} %get-tuple-element.139), channel_id=1, source_target_pairs={{4,0},{8,4},{12,8},{16,12},{20,16},{24,20},{28,24},{32,28},{36,32}... | collective-permute-start | bytes 49160 | tf_op jit(solution)/shard_map/while/body/eval_jaxpr/ppermute | solution.py:24
  406.2 9.8 %collective-permute-start.1 = (f32[1,16,256]{2,1,0:T(8,128)S(1)}, f32[1,16,256]{2,1,0:T(8,128)S(1)}, u32[]{:S(2)}, u32[]{:S(2)}) collective-permute-start(f32[1,16,256]{2,1,0:T(8,128)S(1)} %get-tuple-element.140), channel_id=1, source_target_pairs={{0,4},{4,8},{8,12},{12,16},{16,20},{20,24},{24,28},{28,32},{32,36}... | collective-permute-start | bytes 49160 | tf_op jit(solution)/shard_map/while/body/eval_jaxpr/ppermute | solution.py:21
  417.7 4.4 collective-permute-start.3
  422.2 10.9 %collective-permute-start.5 = (f32[1,16,256]{2,1,0:T(8,128)S(1)}, f32[1,16,256]{2,1,0:T(8,128)S(1)}, u32[]{:S(2)}, u32[]{:S(2)}) collective-permute-start(f32[1,16,256]{2,1,0:T(8,128)S(1)} %get-tuple-element.105), channel_id=1, source_target_pairs={{0,4},{4,8},{8,12},{12,16},{16,20},{20,24},{24,28},{28,32},{32,36}... | collective-permute-start | bytes 49160 | tf_op jit(solution)/shard_map/ppermute | solution.py:21
  431.2 8.4 %collective-permute-start.4 = (f32[1,16,256]{2,1,0:T(8,128)S(1)}, f32[1,16,256]{2,1,0:T(8,128)S(1)}, u32[]{:S(2)}, u32[]{:S(2)}) collective-permute-start(f32[1,16,256]{2,1,0:T(8,128)S(1)} %get-tuple-element.104), channel_id=1, source_target_pairs={{4,0},{8,4},{12,8},{16,12},{20,16},{24,20},{28,24},{32,28},{36,32}... | collective-permute-start | bytes 49160 | tf_op jit(solution)/shard_map/ppermute | solution.py:24
  439.6 5.5 collective-permute-start.6
  440.9 4.8 collective-permute-start.7
  (11 other events, 226.5 us)
Sparse Core Ops, SparseCore 0:
  157.2 47.6 all-reduce.4
  446.8 22.1 all-gather.1
where the time goes:
time: 601 us; the launch traced here: 595 us
  starting transfers between devices  183 us (30%)
  other arithmetic  140 us (23%)
  local copies, waits for them, and re-layouts  133 us (22%)
  waiting for transfers between devices  123 us (20%)
  between operations  15.6 us (3%)
    ppermute x26, starting transfers between devices, extended(): lax.ppermute(lax.slice_in_dim(block, block.shape[dim] - width, None, axis...  137 us
    scatter-add x2, other arithmetic, body(): partial_value = partial_value.at[:, target].add(amounts * grain_weight).a...  119 us
    unnamed x3, waiting for transfers between devices  46.5 us
    ppermute x26, starting transfers between devices, extended(): lax.ppermute(lax.slice_in_dim(block, 0, width, axis=dim), axis, backward)  45.9 us
    ppermute x26, waiting for transfers between devices, extended(): lax.ppermute(lax.slice_in_dim(block, 0, width, axis=dim), axis, backward)  43.2 us
    gather x1, local copies, waits for them, and re-layouts, body(): table[:, source_index + 1]  38.4 us
    gather x1, local copies, waits for them, and re-layouts, body(): table[:, source_index]  38.4 us
    all_gather x1, waiting for transfers between devices, body(): table = lax.all_gather(stacked, 'quad', axis=2, tiled=True)  22.3 us
  transfers between devices with their start and end apart: 54, of which 28 were waited for; matrix products, arithmetic and copies ran while one was open for 0% of the time, Pallas kernels for 0%

commit v1 on v0

v1 whole, which is shorter than its diff:
```python
import functools

import jax
import jax.numpy as jnp
from jax import lax
from jax.experimental import pallas as pl
from jax.experimental.pallas import tpu as pltpu
from jax.sharding import PartitionSpec as P

CH = 4
CA = 16
CB = 256
QUADS = 4
ROWS = CH * CA * QUADS
ACROSS = CA * QUADS
PAD = 8
CHUNK = CB // QUADS
GBLOCK = 1024
GTILE = 256

F32 = jnp.float32
BF16 = jnp.bfloat16


def split(x):
    high = x.astype(BF16)
    return high, (x - high.astype(F32)).astype(BF16)


def row_index(cell):
    return cell[1:2] * ACROSS + cell[0:1] * CA + cell[2:3]


def one_hot_rows(rows, width):
    wanted = lax.broadcasted_iota(jnp.int32, (ROWS, width), 0)
    return jnp.where(wanted == rows, 1.0, 0.0).astype(BF16)


def masses(count_ref, vol, start, width):
    slots = start + lax.broadcasted_iota(jnp.int32, (1, width), 1)
    return jnp.where(slots < count_ref[0], vol, 0.0)


def deposit_kernel(count_ref, cell_ref, weight_ref, volume_ref, velocity_ref, out_ref):
    step = pl.program_id(0)

    @pl.when(step == 0)
    def _():
        out_ref[...] = jnp.zeros_like(out_ref)

    cell = cell_ref[...]
    weight = weight_ref[...]
    mass = masses(count_ref, volume_ref[...], step * GBLOCK, GBLOCK)
    upper = 1.0 - weight
    along = cell[3:4]
    rows = one_hot_rows(row_index(cell), GBLOCK)
    wanted = lax.broadcasted_iota(jnp.int32, (CB, GBLOCK), 0)
    lower_hit = wanted == along
    upper_hit = wanted == along + 1
    for field, amount in enumerate((mass, mass * velocity_ref[0:1])):
        low_hi, low_lo = split(amount * weight)
        up_hi, up_lo = split(amount * upper)
        total = None
        for low, up in ((low_hi, up_hi), (low_lo, up_lo)):
            spread = jnp.where(
                lower_hit, low.astype(F32), jnp.where(upper_hit, up.astype(F32), 0.0)
            ).astype(BF16)
            part = lax.dot_general(
                spread, rows, (((1,), (1,)), ((), ())), preferred_element_type=F32
            )
            total = part if total is None else total + part
        for pair in range(2):
            out_ref[field, pair] += total[:, pair * 128 : (pair + 1) * 128]


def relax_kernel(
    slabs,
    d_ref,
    p_ref,
    s_ref,
    gathered,
    coef,
    a_ref,
    b_ref,
    x0,
    x1,
    y0,
    z0,
    rs_send,
    rs_recv,
    ag_send,
    ag_recv,
    halo_send,
    halo_recv,
    p_send,
    p_recv,
):
    quad = lax.axis_index("quad")
    slab = lax.axis_index("slab")
    nexts = lax.rem(slab + 1, slabs)
    prevs = lax.rem(slab + slabs - 1, slabs)
    peers = [lax.rem(quad + d, QUADS) for d in range(QUADS)]
    origins = [lax.rem(quad + QUADS - d, QUADS) for d in range(QUADS)]

    def at(q, s):
        return {"quad": q, "slab": s}

    def rows_of(q):
        return pl.ds(pl.multiple_of(q * CHUNK, CHUNK), CHUNK)

    barrier = pltpu.get_barrier_semaphore()
    partners = [at(peers[d], slab) for d in range(1, QUADS)]
    partners += [at(quad, nexts), at(quad, prevs)]
    for partner in partners:
        pl.semaphore_signal(
            barrier, inc=1, device_id=partner, device_id_type=pl.DeviceIdType.MESH
        )
    for buffer in (x0, x1, y0, z0, p_ref):
        zero = jnp.zeros((buffer.shape[0], PAD, 128), F32)
        buffer[:, 0:PAD, :] = zero
        buffer[:, PAD + CB :, :] = zero
    pl.semaphore_wait(barrier, len(partners))

    def send(src, dst, ssem, rsem, where):
        copy = pltpu.make_async_remote_copy(
            src_ref=src,
            dst_ref=dst,
            send_sem=ssem,
            recv_sem=rsem,
            device_id=where,
            device_id_type=pl.DeviceIdType.MESH,
        )
        copy.start()
        return copy

    scatter = []
    for d in (2, 1, 3):
        scatter.append(
            send(
                d_ref.at[:, :, rows_of(peers[d]), :],
                gathered.at[d - 1],
                rs_send.at[d - 1],
                rs_recv.at[d - 1],
                at(peers[d], slab),
            )
        )
    own = rows_of(quad)
    for copy in scatter:
        copy.wait_recv()
    coef[:, 2:4, own, :] = (d_ref[:, :, own, :] + gathered[0]) + (gathered[1] + gathered[2])

    mine = coef.at[:, 2:4, own, :]
    gather = {}
    for d in (2, 1, 3):
        gather[d] = send(mine, mine, ag_send.at[d - 1], ag_recv.at[d - 1], at(peers[d], slab))
    halos = []

    def forward(d):
        block = rows_of(origins[d])
        src = coef.at[:, 2:4, block, :]
        halos.append(
            send(src, coef.at[:, 0:2, block, :], halo_send.at[0, d], halo_recv.at[0, d], at(quad, nexts))
        )
        halos.append(
            send(src, coef.at[:, 4:6, block, :], halo_send.at[1, d], halo_recv.at[1, d], at(quad, prevs))
        )

    forward(0)
    for d in (1, 3, 2):
        gather[d].wait_recv()
        forward(d)
    for copy in halos:
        copy.wait_recv()

    not_first = jnp.where(slab > 0, 1.0, 0.0)
    not_last = jnp.where(slab < slabs - 1, 1.0, 0.0)

    def coefficients(k, carry):
        live = jnp.where(k < 2, not_first, jnp.where(k > 3, not_last, 1.0))
        for r in range(0, CB, 64):
            thick = 1.0 + coef[0, k, r : r + 64, :]
            ratio = live / (6.0 + 0.05 * thick)
            source = 4.0 * coef[1, k, r : r + 64, :] * thick * ratio
            b_ref[k, r : r + 64, :] = ratio
            a_ref[k, r : r + 64, :] = source
            x0[k, PAD + r : PAD + r + 64, :] = source
        return carry

    lax.fori_loop(0, 6, coefficients, 0)
    for k in range(2):
        s_ref[k] = coef[0, 2 + k]

    lane = lax.broadcasted_iota(jnp.int32, (64, 128), 1)
    second = lane >= 64
    place = lax.rem(lane, 64)
    has_low = place > 0
    has_high = place < 63

    def sweep(src, dst, start, stop, shift=0):
        def body(k, carry):
            below = jnp.maximum(k - 1, 0)
            above = jnp.minimum(k + 1, 5)
            for r in range(0, CB, 64):
                o = PAD + r
                here = src[k, o : o + 64, :]
                layers = here + jnp.where(second, src[below, o : o + 64, :], src[above, o : o + 64, :])
                total = pltpu.roll(layers, 64, axis=1)
                total += src[k, o - 1 : o + 63, :] + src[k, o + 1 : o + 65, :]
                total += jnp.where(has_low, pltpu.roll(here, 1, axis=1), 0.0)
                total += jnp.where(has_high, pltpu.roll(here, 127, axis=1), 0.0)
                dst[k - shift, o : o + 64, :] = (
                    a_ref[k, r : r + 64, :] + b_ref[k, r : r + 64, :] * total
                )
            return carry

        lax.fori_loop(start, stop, body, 0)

    def exchange(buffer, n):
        src = buffer.at[2:4, PAD : PAD + CB, :]
        copies = [
            send(src, buffer.at[0:2, PAD : PAD + CB, :], p_send.at[n, 0], p_recv.at[n, 0], at(quad, nexts)),
            send(src, buffer.at[4:6, PAD : PAD + CB, :], p_send.at[n, 1], p_recv.at[n, 1], at(quad, prevs)),
        ]
        for copy in copies:
            copy.wait_recv()

        @pl.when(slab == 0)
        def _():
            buffer[0:2, PAD : PAD + CB, :] = jnp.zeros((2, CB, 128), F32)

        @pl.when(slab == slabs - 1)
        def _():
            buffer[4:6, PAD : PAD + CB, :] = jnp.zeros((2, CB, 128), F32)

        return copies

    sweep(x0, x1, 0, 6)
    sweep(x1, x0, 1, 5)
    sweep(x0, x1, 1, 5)
    sweep(x1, y0, 2, 4)
    first = exchange(y0, 0)
    sweep(y0, x0, 0, 6)
    sweep(x0, x1, 1, 5)
    sweep(x1, x0, 1, 5)
    sweep(x0, z0, 2, 4)
    later = exchange(z0, 1)
    sweep(z0, x0, 0, 6)
    sweep(x0, x1, 1, 5)
    sweep(x1, p_ref, 1, 5, shift=1)

    for copy in scatter + list(gather.values()) + halos + first + later:
        copy.wait_send()


def sample_kernel(
    count_ref,
    cell_ref,
    weight_ref,
    volume_ref,
    velocity_ref,
    p_ref,
    s_ref,
    pressure_ref,
    drag_ref,
    high_ref,
    low_ref,
    turned,
):
    step = pl.program_id(0)

    @pl.when(step == 0)
    def _():
        lane = lax.broadcasted_iota(jnp.int32, (CB, 128), 1)
        first = lane < 64
        place = lax.rem(lane, 64)
        for k in range(2):
            rows = slice(PAD, PAD + CB)
            here = p_ref[k + 1, rows, :]
            swap = [pltpu.roll(p_ref[k + j, rows, :], 64, axis=1) for j in range(3)]
            high = jnp.where(first, swap[1], swap[2])
            low = jnp.where(first, swap[0], swap[1])
            fields = [-0.5 * (high - low)]
            right = jnp.where(place < 63, pltpu.roll(here, 127, axis=1), 0.0)
            left = jnp.where(place > 0, pltpu.roll(here, 1, axis=1), 0.0)
            fields.append(-0.5 * (right - left))
            fields.append(
                -0.5 * (p_ref[k + 1, PAD + 1 : PAD + CB + 1, :] - p_ref[k + 1, PAD - 1 : PAD + CB - 1, :])
            )
            fields.append(s_ref[k])
            for f, field in enumerate(fields):
                hi, lo = split(field)
                high_ref[f * CB : (f + 1) * CB, k * 128 : (k + 1) * 128] = hi
                low_ref[f * CB : (f + 1) * CB, k * 128 : (k + 1) * 128] = lo
            turned[k * 128 : (k + 1) * 128, :] = here.T
        quad = lax.axis_index("quad")
        for layer in range(CH):
            at = pl.multiple_of(layer * ACROSS + quad * CA, CA)
            pressure_ref[layer] = turned[pl.ds(at, CA), :]

    def body(t, carry):
        base = pl.multiple_of(t * GTILE, GTILE)
        tile = pl.ds(base, GTILE)
        cell = cell_ref[:, tile]
        weight = weight_ref[:, tile]
        upper = 1.0 - weight
        mass = masses(count_ref, volume_ref[:, tile], step * GBLOCK + base, GTILE)
        rows = one_hot_rows(row_index(cell), GTILE)
        along = cell[3:4]
        wanted = lax.broadcasted_iota(jnp.int32, (CB, GTILE), 0)
        pick = jnp.where(wanted == along, weight, jnp.where(wanted == along + 1, upper, 0.0))
        sampled = []
        for f in range(4):
            block = slice(f * CB, (f + 1) * CB)
            picked = jnp.dot(high_ref[block, :], rows, preferred_element_type=F32)
            picked += jnp.dot(low_ref[block, :], rows, preferred_element_type=F32)
            sampled.append(jnp.sum(pick * picked, axis=0, keepdims=True))
        factor = mass * (1.0 + sampled[3]) ** 2
        for f in range(3):
            drag_ref[f : f + 1, tile] = factor * (sampled[f] - velocity_ref[f : f + 1, tile])
        return carry

    lax.fori_loop(0, GBLOCK // GTILE, body, 0)


def body(slabs, grain_cell, grain_count, grain_weight, grain_volume, grain_velocity):
    grains = grain_weight.shape[0]
    weight = grain_weight.reshape(1, grains)
    volume = grain_volume.reshape(1, grains)
    smem = pl.BlockSpec(memory_space=pltpu.SMEM)
    vmem = pl.BlockSpec(memory_space=pltpu.VMEM)
    grain_specs = [
        smem,
        pl.BlockSpec((4, GBLOCK), lambda i: (0, i)),
        pl.BlockSpec((1, GBLOCK), lambda i: (0, i)),
        pl.BlockSpec((1, GBLOCK), lambda i: (0, i)),
        pl.BlockSpec((3, GBLOCK), lambda i: (0, i)),
    ]
    steps = grains // GBLOCK
    deposits = pl.pallas_call(
        deposit_kernel,
        grid=(steps,),
        out_shape=jax.ShapeDtypeStruct((2, 2, CB, 128), F32),
        in_specs=grain_specs,
        out_specs=pl.BlockSpec((2, 2, CB, 128), lambda i: (0, 0, 0, 0)),
        name="deposit",
    )(grain_count, grain_cell, weight, volume, grain_velocity)
    dma = pltpu.SemaphoreType.DMA
    pressure, solid = pl.pallas_call(
        functools.partial(relax_kernel, slabs),
        out_shape=(
            jax.ShapeDtypeStruct((4, CB + 2 * PAD, 128), F32),
            jax.ShapeDtypeStruct((2, CB, 128), F32),
        ),
        in_specs=[vmem],
        out_specs=(vmem, vmem),
        scratch_shapes=[
            pltpu.VMEM((3, 2, 2, CHUNK, 128), F32),
            pltpu.VMEM((2, 6, CB, 128), F32),
            pltpu.VMEM((6, CB, 128), F32),
            pltpu.VMEM((6, CB, 128), F32),
        ]
        + [pltpu.VMEM((6, CB + 2 * PAD, 128), F32)] * 4
        + [dma((3,))] * 4
        + [dma((2, QUADS))] * 2
        + [dma((2, 2))] * 2,
        compiler_params=pltpu.CompilerParams(collective_id=0, has_side_effects=True),
        name="relax",
    )(deposits)
    return pl.pallas_call(
        sample_kernel,
        grid=(steps,),
        out_shape=(
            jax.ShapeDtypeStruct((CH, CA, CB), F32),
            jax.ShapeDtypeStruct((3, grains), F32),
        ),
        in_specs=grain_specs + [vmem, vmem],
        out_specs=(
            pl.BlockSpec((CH, CA, CB), lambda i: (0, 0, 0)),
            pl.BlockSpec((3, GBLOCK), lambda i: (0, i)),
        ),
        scratch_shapes=[
            pltpu.VMEM((4 * CB, ROWS), BF16),
            pltpu.VMEM((4 * CB, ROWS), BF16),
            pltpu.VMEM((ROWS, CB), F32),
        ],
        name="sample",
    )(grain_count, grain_cell, weight, volume, grain_velocity, pressure, solid)


def solution(mesh):
    placed = (
        P(None, ("slab", "quad")),
        P(("slab", "quad")),
        P(("slab", "quad")),
        P(("slab", "quad")),
        P(None, ("slab", "quad")),
    )
    return jax.shard_map(
        functools.partial(body, mesh.shape["slab"]),
        mesh=mesh,
        in_specs=placed,
        out_specs=(P("slab", "quad", None), P(None, ("slab", "quad"))),
        check_vma=False,
    )
```

time: 601 us -> 82.9 us (0.14)
  the two profiles are of different devices: /device:TPU:121 before, /device:TPU:2 now
where the time goes in v1:
time: 82.9 us; the launch traced here: 82.7 us
  Pallas kernels  81.4 us (98%)
  between operations  1.28 us (2%)
    pallas_call x1, Pallas kernels, body(): pl.pallas_call(functools.partial(relax_kernel, slabs), out_shape=(jax.Sha...  53.9 us
    pallas_call x1, Pallas kernels, body(): pl.pallas_call(sample_kernel, grid=(steps,), out_shape=(jax.ShapeDtypeStr...  17.7 us
    pallas_call x1, Pallas kernels, body(): pl.pallas_call(deposit_kernel, grid=(steps,), out_shape=jax.ShapeDtypeStr...  9.79 us

profile of v1, /device:TPU:2, one launch (start us, length us, event | category | flops | bytes accessed | tf_op | source)
XLA Modules:
  0.0 82.7 jit_solution(17803209537600061684)
XLA Ops:
  1.3 9.8 %deposit.1.d_ref = f32[2,2,256,128]{3,2,1,0:T(8,128)} custom-call(s32[1]{0:T(128)S(6)} %copy.7.count_ref, s32[4,8192]{1,0:T(4,128)} %cell_ref.3, f32[1,8192]{1,0:T(1,128)} %bitcast.2, f32[1,8192]{1,0:T(1,128)} %bitcast.4, f32[3,8192]{1,0:T(4,128)} %velocity_ref.3), custom_call_target="tpu_custom_call" | custom-call | tf_op jit(solution)/shard_map/deposit/pallas_call | solution.py:339
  11.1 53.9 %relax.1 = (f32[4,272,128]{2,1,0:T(8,128)}, f32[2,256,128]{2,1,0:T(8,128)}) custom-call(f32[2,2,256,128]{3,2,1,0:T(8,128)} %deposit.1.d_ref), custom_call_target="tpu_custom_call" | custom-call | tf_op jit(solution)/shard_map/relax/pallas_call | solution.py:348
  65.0 17.7 %sample.1 = (f32[4,16,256]{2,1,0:T(8,128)}, f32[3,8192]{1,0:T(4,128)}) custom-call(s32[1]{0:T(128)S(6)} %copy.7.count_ref, s32[4,8192]{1,0:T(4,128)} %cell_ref.3, f32[1,8192]{1,0:T(1,128)} %bitcast.3, f32[1,8192]{1,0:T(1,128)} %bitcast.5, f32[3,8192]{1,0:T(4,128)} %velocity_ref.3, f32[4,272,128]{2,1,0:T(8,128)} %get-tuple-element.4.p_ref, ...), custom_call_target="tpu_custom_call" | custom-call | tf_op jit(solution)/shard_map/sample/pallas_call | solution.py:369

commit v2 on v1

v2 whole, which is shorter than its diff:
```python
import functools

import jax
import jax.numpy as jnp
from jax import lax
from jax.experimental import pallas as pl
from jax.experimental.pallas import tpu as pltpu
from jax.sharding import PartitionSpec as P

CH = 4
CA = 16
CB = 256
QUADS = 4
ROWS = CH * CA * QUADS
ACROSS = CA * QUADS
PAD = 8
HALF = CB // 2
HELD = HALF + 2 * PAD
CHUNK = HALF // QUADS
GBLOCK = 1024
GTILE = 512
UNROLL = 4

F32 = jnp.float32
BF16 = jnp.bfloat16


def split(x):
    high = x.astype(BF16)
    return high, (x - high.astype(F32)).astype(BF16)


def row_index(cell):
    return cell[1:2] * ACROSS + cell[0:1] * CA + cell[2:3]


def small(x):
    return x.astype(F32).astype(BF16)


def one_hot_rows(rows, width):
    wanted = small(lax.broadcasted_iota(jnp.int32, (ROWS, width), 0))
    return jnp.where(wanted == small(rows), BF16(1.0), BF16(0.0))


def masses(count_ref, vol, start, width):
    slots = start + lax.broadcasted_iota(jnp.int32, (1, width), 1)
    return jnp.where(slots < count_ref[0], vol, 0.0)


def fold(top, bottom, first):
    return (
        jnp.where(first, top, pltpu.roll(bottom, 64, axis=1)),
        jnp.where(first, pltpu.roll(top, 64, axis=1), bottom),
    )


def deposit(count_ref, cell_ref, weight_ref, volume_ref, velocity_ref, out_ref, total, va, vb):
    total[...] = jnp.zeros_like(total)
    blocks = cell_ref.shape[1] // GBLOCK

    def tile_of(t):
        return pl.ds(pl.multiple_of(t * GBLOCK, GBLOCK), GBLOCK)

    def build(t, spread):
        tile = tile_of(t)
        weight = weight_ref[:, tile]
        mass = masses(count_ref, volume_ref[:, tile], t * GBLOCK, GBLOCK)
        upper = 1.0 - weight
        along = small(cell_ref[3:4, tile])
        above = along + BF16(1.0)
        shares = []
        for amount in (mass, mass * velocity_ref[0:1, tile]):
            shares += zip(split(amount * weight), split(amount * upper))
        for r in range(0, CB, 16):
            wanted = small(lax.broadcasted_iota(jnp.int32, (16, GBLOCK), 0) + r)
            lower_hit = wanted == along
            upper_hit = wanted == above
            for n, (low, up) in enumerate(shares):
                spread[n * CB + r : n * CB + r + 16, :] = jnp.where(
                    lower_hit, low, jnp.where(upper_hit, up, BF16(0.0))
                )

    def add(t, spread):
        rows = one_hot_rows(row_index(cell_ref[:, tile_of(t)]), GBLOCK)
        total[...] += lax.dot_general(
            spread[...], rows, (((1,), (1,)), ((), ())), preferred_element_type=F32
        )

    build(0, va)

    def body(i, carry):
        t = 2 * i
        build(t + 1, vb)
        add(t, va)
        build(jnp.minimum(t + 2, blocks - 1), va)
        add(t + 1, vb)
        return carry

    lax.fori_loop(0, blocks // 2, body, 0)
    first = lax.broadcasted_iota(jnp.int32, (HALF, 128), 1) < 64
    for field in range(2):
        for pair in range(2):
            lanes = slice(pair * 128, (pair + 1) * 128)
            r = field * 2 * CB
            whole = total[r : r + CB, lanes] + total[r + CB : r + 2 * CB, lanes]
            even, odd = fold(whole[:HALF], whole[HALF:], first)
            out_ref[field, 2 * pair] = even
            out_ref[field, 2 * pair + 1] = odd


def relax_kernel(
    slabs,
    count_ref,
    cell_ref,
    weight_ref,
    volume_ref,
    velocity_ref,
    p_ref,
    solid_ref,
    d_ref,
    total_ref,
    va,
    vb,
    high_ref,
    low_ref,
    gathered,
    coef,
    a_ref,
    b_ref,
    x0,
    x1,
    y0,
    z0,
    rs_send,
    rs_recv,
    ag_send,
    ag_recv,
    halo_send,
    halo_recv,
    p_send,
    p_recv,
):
    quad = lax.axis_index("quad")
    slab = lax.axis_index("slab")
    nexts = lax.rem(slab + 1, slabs)
    prevs = lax.rem(slab + slabs - 1, slabs)
    peers = [lax.rem(quad + d, QUADS) for d in range(QUADS)]
    origins = [lax.rem(quad + QUADS - d, QUADS) for d in range(QUADS)]

    def at(q, s):
        return {"quad": q, "slab": s}

    def rows_of(q):
        return pl.ds(pl.multiple_of(q * CHUNK, CHUNK), CHUNK)

    barrier = pltpu.get_barrier_semaphore()
    partners = [at(peers[d], slab) for d in range(1, QUADS)]
    partners += [at(quad, nexts), at(quad, prevs)]
    for partner in partners:
        pl.semaphore_signal(
            barrier, inc=1, device_id=partner, device_id_type=pl.DeviceIdType.MESH
        )
    deposit(count_ref, cell_ref, weight_ref, volume_ref, velocity_ref, d_ref, total_ref, va, vb)
    pl.semaphore_wait(barrier, len(partners))

    def send(src, dst, ssem, rsem, where):
        copy = pltpu.make_async_remote_copy(
            src_ref=src,
            dst_ref=dst,
            send_sem=ssem,
            recv_sem=rsem,
            device_id=where,
            device_id_type=pl.DeviceIdType.MESH,
        )
        copy.start()
        return copy

    scatter, gather, halos = [], [], []
    for f in range(2):
        scatter.append(
            {
                d: send(
                    d_ref.at[f, :, rows_of(peers[d]), :],
                    gathered.at[f, d - 1],
                    rs_send.at[f, d - 1],
                    rs_recv.at[f, d - 1],
                    at(peers[d], slab),
                )
                for d in (2, 1, 3)
            }
        )
    own = rows_of(quad)

    def forward(f, d):
        block = rows_of(origins[d])
        src = coef.at[f, 4:8, block, :]
        for side, (low, where) in enumerate(((0, nexts), (8, prevs))):
            halos.append(
                send(
                    src,
                    coef.at[f, low : low + 4, block, :],
                    halo_send.at[f, side, d],
                    halo_recv.at[f, side, d],
                    at(quad, where),
                )
            )

    for f in range(2):
        for copy in scatter[f].values():
            copy.wait_recv()
        coef[f, 4:8, own, :] = (d_ref[f, :, own, :] + gathered[f, 0]) + (
            gathered[f, 1] + gathered[f, 2]
        )
        mine = coef.at[f, 4:8, own, :]
        gather.append(
            {
                d: send(mine, mine, ag_send.at[f, d - 1], ag_recv.at[f, d - 1], at(peers[d], slab))
                for d in (2, 1, 3)
            }
        )
        forward(f, 0)
    for f in range(2):
        for d in (1, 3, 2):
            gather[f][d].wait_recv()
            forward(f, d)

    first = lax.broadcasted_iota(jnp.int32, (HALF, 128), 1) < 64
    for pair in range(2):
        store_split(fold(coef[0, 4 + 2 * pair], coef[0, 5 + 2 * pair], first), high_ref, low_ref, 0, pair)

    def keep(tile, sampled):
        solid_ref[:, tile] = sampled[0]

    sample(cell_ref, weight_ref, high_ref, low_ref, 1, keep)
    for copy in halos:
        copy.wait_recv()

    not_first = jnp.where(slab > 0, 1.0, 0.0)
    not_last = jnp.where(slab < slabs - 1, 1.0, 0.0)

    lane = lax.broadcasted_iota(jnp.int32, (HALF, 128), 1)
    place = lax.rem(lane, 64)
    has_low = place > 0
    has_high = place < 63
    second = lax.broadcasted_iota(jnp.int32, (1, 128), 1) >= 64

    def put(dst, k, value):
        dst[k, PAD : PAD + HALF, :] = value
        dst[k, PAD - 1 : PAD, :] = jnp.where(second, pltpu.roll(value[HALF - 1 :], 64, axis=1), 0.0)
        dst[k, PAD + HALF : PAD + HALF + 1, :] = jnp.where(
            second, 0.0, pltpu.roll(value[:1], 64, axis=1)
        )

    def coefficients(k, carry):
        live = jnp.where(k < 4, not_first, jnp.where(k > 7, not_last, 1.0))
        thick = 1.0 + coef[0, k]
        ratio = live / (6.0 + 0.05 * thick)
        source = 4.0 * coef[1, k] * thick * ratio
        b_ref[k] = ratio
        a_ref[k] = source
        put(x0, k, source)
        return carry

    lax.fori_loop(0, 12, coefficients, 0)
    def sweep(src, dst, start, stop, shift=0):
        def body(i, carry):
            for k in (start + 2 * i, start + 2 * i + 1):
                here = src[k, PAD : PAD + HALF, :]
                total = src[k - 1, PAD : PAD + HALF, :] + src[k + 1, PAD : PAD + HALF, :]
                total += src[k, PAD - 1 : PAD + HALF - 1, :] + src[k, PAD + 1 : PAD + HALF + 1, :]
                total += jnp.where(has_low, pltpu.roll(here, 1, axis=1), 0.0)
                total += jnp.where(has_high, pltpu.roll(here, 127, axis=1), 0.0)
                put(dst, k - shift, a_ref[k] + b_ref[k] * total)
            return carry

        lax.fori_loop(0, (stop - start) // 2, body, 0)

    def exchange(buffer, n):
        src = buffer.at[4:8]
        copies = [
            send(src, buffer.at[0:4], p_send.at[n, 0], p_recv.at[n, 0], at(quad, nexts)),
            send(src, buffer.at[8:12], p_send.at[n, 1], p_recv.at[n, 1], at(quad, prevs)),
        ]
        for copy in copies:
            copy.wait_recv()

        @pl.when(slab == 0)
        def _():
            buffer[0:4] = jnp.zeros((4, HELD, 128), F32)

        @pl.when(slab == slabs - 1)
        def _():
            buffer[8:12] = jnp.zeros((4, HELD, 128), F32)

        return copies

    sweep(x0, x1, 1, 11)
    sweep(x1, x0, 2, 10)
    sweep(x0, x1, 3, 9)
    sweep(x1, y0, 4, 8)
    early = exchange(y0, 0)
    sweep(y0, x0, 1, 11)
    sweep(x0, x1, 2, 10)
    sweep(x1, x0, 3, 9)
    sweep(x0, z0, 4, 8)
    later = exchange(z0, 1)
    sweep(z0, x0, 1, 11)
    sweep(x0, x1, 2, 10)
    sweep(x1, p_ref, 3, 9, shift=3)

    for copies in scatter + gather:
        for copy in copies.values():
            copy.wait_send()
    for copy in halos + early + later:
        copy.wait_send()


def store_split(halves, high_ref, low_ref, f, pair):
    for h, half in enumerate(halves):
        hi, lo = split(half)
        r = f * CB + h * HALF
        high_ref[r : r + HALF, pair * 128 : (pair + 1) * 128] = hi
        low_ref[r : r + HALF, pair * 128 : (pair + 1) * 128] = lo


def sample(cell_ref, weight_ref, high_ref, low_ref, fields, done):
    def one(base):
        tile = pl.ds(base, GTILE)
        rows = one_hot_rows(row_index(cell_ref[:, tile]), GTILE)
        weight = weight_ref[:, tile]
        upper = 1.0 - weight
        along = cell_ref[3:4, tile]
        wanted = lax.broadcasted_iota(jnp.int32, (CB, GTILE), 0)
        pick = jnp.where(wanted == along, weight, jnp.where(wanted == along + 1, upper, 0.0))
        picked = jnp.dot(high_ref[...], rows, preferred_element_type=F32)
        picked += jnp.dot(low_ref[...], rows, preferred_element_type=F32)
        done(
            tile,
            [
                jnp.sum(pick * picked[f * CB : (f + 1) * CB], axis=0, keepdims=True)
                for f in range(fields)
            ],
        )

    def body(i, carry):
        for j in range(UNROLL):
            one(pl.multiple_of((i * UNROLL + j) * GTILE, GTILE))
        return carry

    lax.fori_loop(0, cell_ref.shape[1] // (GTILE * UNROLL), body, 0)


def sample_kernel(
    count_ref,
    cell_ref,
    weight_ref,
    volume_ref,
    velocity_ref,
    p_ref,
    solid_ref,
    pressure_ref,
    drag_ref,
    high_ref,
    low_ref,
    turned,
):
    lane = lax.broadcasted_iota(jnp.int32, (HALF, 128), 1)
    first = lane < 64
    place = lax.rem(lane, 64)
    inner = slice(PAD, PAD + HALF)
    for pair in range(2):
        layers = []
        for k in (2 * pair, 2 * pair + 1):
            here = p_ref[k + 1, inner, :]
            fields = [-0.5 * (p_ref[k + 2, inner, :] - p_ref[k, inner, :])]
            right = jnp.where(place < 63, pltpu.roll(here, 127, axis=1), 0.0)
            left = jnp.where(place > 0, pltpu.roll(here, 1, axis=1), 0.0)
            fields.append(-0.5 * (right - left))
            fields.append(
                -0.5
                * (p_ref[k + 1, PAD + 1 : PAD + HALF + 1, :] - p_ref[k + 1, PAD - 1 : PAD + HALF - 1, :])
            )
            layers.append(fields)
            turned[k] = here.T
        for f in range(3):
            store_split(fold(layers[0][f], layers[1][f], first), high_ref, low_ref, f, pair)
    quad = lax.axis_index("quad")
    for layer in range(CH):
        for h in range(2):
            at = pl.multiple_of(h * 64 + quad * CA, CA)
            pressure_ref[layer, :, h * HALF : (h + 1) * HALF] = turned[layer, pl.ds(at, CA), :]

    def finish(tile, sampled):
        slots = tile.start + lax.broadcasted_iota(jnp.int32, (1, GTILE), 1)
        mass = jnp.where(slots < count_ref[0], volume_ref[:, tile], 0.0)
        factor = mass * (1.0 + solid_ref[:, tile]) ** 2
        for f in range(3):
            drag_ref[f : f + 1, tile] = factor * (sampled[f] - velocity_ref[f : f + 1, tile])

    sample(cell_ref, weight_ref, high_ref, low_ref, 3, finish)


def body(slabs, grain_cell, grain_count, grain_weight, grain_volume, grain_velocity):
    grains = grain_weight.shape[0]
    weight = grain_weight.reshape(1, grains)
    volume = grain_volume.reshape(1, grains)
    smem = pl.BlockSpec(memory_space=pltpu.SMEM)
    vmem = pl.BlockSpec(memory_space=pltpu.VMEM)
    dma = pltpu.SemaphoreType.DMA
    pressure, solid = pl.pallas_call(
        functools.partial(relax_kernel, slabs),
        out_shape=(
            jax.ShapeDtypeStruct((CH + 2, HELD, 128), F32),
            jax.ShapeDtypeStruct((1, grains), F32),
        ),
        in_specs=[smem, vmem, vmem, vmem, vmem],
        out_specs=(vmem, vmem),
        scratch_shapes=[
            pltpu.VMEM((2, CH, HALF, 128), F32),
            pltpu.VMEM((4 * CB, ROWS), F32),
            pltpu.VMEM((4 * CB, GBLOCK), BF16),
            pltpu.VMEM((4 * CB, GBLOCK), BF16),
            pltpu.VMEM((CB, ROWS), BF16),
            pltpu.VMEM((CB, ROWS), BF16),
            pltpu.VMEM((2, 3, CH, CHUNK, 128), F32),
            pltpu.VMEM((2, 3 * CH, HALF, 128), F32),
            pltpu.VMEM((3 * CH, HALF, 128), F32),
            pltpu.VMEM((3 * CH, HALF, 128), F32),
        ]
        + [pltpu.VMEM((3 * CH, HELD, 128), F32)] * 4
        + [dma((2, 3))] * 4
        + [dma((2, 2, QUADS))] * 2
        + [dma((2, 2))] * 2,
        compiler_params=pltpu.CompilerParams(collective_id=0, has_side_effects=True),
        name="relax",
    )(grain_count, grain_cell, weight, volume, grain_velocity)
    return pl.pallas_call(
        sample_kernel,
        out_shape=(
            jax.ShapeDtypeStruct((CH, CA, CB), F32),
            jax.ShapeDtypeStruct((3, grains), F32),
        ),
        in_specs=[smem] + [vmem] * 6,
        out_specs=(vmem, vmem),
        scratch_shapes=[
            pltpu.VMEM((3 * CB, ROWS), BF16),
            pltpu.VMEM((3 * CB, ROWS), BF16),
            pltpu.VMEM((CH, 128, HALF), F32),
        ],
        name="sample",
    )(grain_count, grain_cell, weight, volume, grain_velocity, pressure, solid)


def solution(mesh):
    placed = (
        P(None, ("slab", "quad")),
        P(("slab", "quad")),
        P(("slab", "quad")),
        P(("slab", "quad")),
        P(None, ("slab", "quad")),
    )
    return jax.shard_map(
        functools.partial(body, mesh.shape["slab"]),
        mesh=mesh,
        in_specs=placed,
        out_specs=(P("slab", "quad", None), P(None, ("slab", "quad"))),
        check_vma=False,
    )
```

time: 82.9 us -> 65 us (0.78)
  the two profiles are of different devices: /device:TPU:2 before, /device:TPU:0 now
where the time goes in v2:
time: 65 us; the launch traced here: 64.8 us
  Pallas kernels  63.5 us (98%)
  between operations  1.28 us (2%)
    pallas_call x1, Pallas kernels, body(): pl.pallas_call(functools.partial(relax_kernel, slabs), out_shape=(jax.Sha...  53.3 us
    pallas_call x1, Pallas kernels, body(): pl.pallas_call(sample_kernel, out_shape=(jax.ShapeDtypeStruct((CH, CA, CB...  10.2 us

profile of v2, /device:TPU:0, one launch (start us, length us, event | category | flops | bytes accessed | tf_op | source)
XLA Modules:
  0.0 64.8 jit_solution(11489174521040593837)
XLA Ops:
  1.3 53.3 %relax.1 = (f32[6,144,128]{2,1,0:T(8,128)}, f32[1,8192]{1,0:T(1,128)}) custom-call(s32[1]{0:T(128)S(6)} %copy.7.count_ref, s32[4,8192]{1,0:T(4,128)} %cell_ref.3, f32[1,8192]{1,0:T(1,128)} %bitcast.2, f32[1,8192]{1,0:T(1,128)} %bitcast.4, f32[3,8192]{1,0:T(4,128)} %velocity_ref.3), custom_call_target="tpu_custom_call" | custom-call | tf_op jit(solution)/shard_map/relax/pallas_call | solution.py:411
  54.6 10.2 %sample.1 = (f32[4,16,256]{2,1,0:T(8,128)}, f32[3,8192]{1,0:T(4,128)}) custom-call(s32[1]{0:T(128)S(6)} %copy.7.count_ref, s32[4,8192]{1,0:T(4,128)} %cell_ref.3, f32[1,8192]{1,0:T(1,128)} %bitcast.3, f32[1,8192]{1,0:T(1,128)} %bitcast.5, f32[3,8192]{1,0:T(4,128)} %velocity_ref.3, f32[6,144,128]{2,1,0:T(8,128)} %get-tuple-element.4.p_ref, ...), custom_call_target="tpu_custom_call" | custom-call | tf_op jit(solution)/shard_map/sample/pallas_call | solution.py:438

commit v3 on v2

v3 whole, which is shorter than its diff:
```python
import functools

import jax
import jax.numpy as jnp
from jax import lax
from jax.experimental import pallas as pl
from jax.experimental.pallas import tpu as pltpu
from jax.sharding import PartitionSpec as P

CH = 4
CA = 16
CB = 256
QUADS = 4
ROWS = CH * CA * QUADS
ACROSS = CA * QUADS
PAD = 8
HALF = CB // 2
HELD = ACROSS + 2 * PAD
GBLOCK = 1024
GTILE = 512
UNROLL = 4

F32 = jnp.float32
BF16 = jnp.bfloat16


def split(x):
    high = x.astype(BF16)
    return high, (x - high.astype(F32)).astype(BF16)


def row_index(cell):
    return cell[1:2] * ACROSS + cell[0:1] * CA + cell[2:3]


def small(x):
    return x.astype(F32).astype(BF16)


def one_hot_rows(rows, width):
    wanted = small(lax.broadcasted_iota(jnp.int32, (ROWS, width), 0))
    return jnp.where(wanted == small(rows), BF16(1.0), BF16(0.0))


def masses(count_ref, vol, start, width):
    slots = start + lax.broadcasted_iota(jnp.int32, (1, width), 1)
    return jnp.where(slots < count_ref[0], vol, 0.0)


def keys(cell):
    along = cell[3:4]
    above = along + 1

    def key(x):
        return (x & 1) * HALF + (x >> 1)

    return key(along), key(above)


def deposit(field, count_ref, cell_ref, weight_ref, volume_ref, velocity_ref, out_ref, total, va, vb):
    total[...] = jnp.zeros_like(total)
    blocks = cell_ref.shape[1] // GBLOCK

    def tile_of(t):
        return pl.ds(pl.multiple_of(t * GBLOCK, GBLOCK), GBLOCK)

    def build(t, spread):
        tile = tile_of(t)
        weight = weight_ref[:, tile]
        amount = masses(count_ref, volume_ref[:, tile], t * GBLOCK, GBLOCK)
        if field:
            amount = amount * velocity_ref[0:1, tile]
        along, above = (small(x) for x in keys(cell_ref[:, tile]))
        shares = list(zip(split(amount * weight), split(amount * (1.0 - weight))))
        for r in range(0, CB, 16):
            wanted = small(lax.broadcasted_iota(jnp.int32, (16, GBLOCK), 0) + r)
            lower_hit = wanted == along
            upper_hit = wanted == above
            for n, (low, up) in enumerate(shares):
                spread[n * CB + r : n * CB + r + 16, :] = jnp.where(
                    lower_hit, low, jnp.where(upper_hit, up, BF16(0.0))
                )

    def add(t, spread):
        rows = one_hot_rows(row_index(cell_ref[:, tile_of(t)]), GBLOCK)
        total[...] += lax.dot_general(
            spread[...], rows, (((1,), (1,)), ((), ())), preferred_element_type=F32
        )

    build(0, va)

    def body(i, carry):
        t = 2 * i
        build(t + 1, vb)
        add(t, va)
        build(jnp.minimum(t + 2, blocks - 1), va)
        add(t + 1, vb)
        return carry

    lax.fori_loop(0, blocks // 2, body, 0)
    for pair in range(2):
        lanes = slice(pair * 128, (pair + 1) * 128)
        whole = total[:CB, lanes] + total[CB:, lanes]
        for odd in range(2):
            block = whole[odd * HALF : (odd + 1) * HALF].T
            for j in range(2):
                out_ref[field, 2 * pair + j, odd] = block[j * ACROSS : (j + 1) * ACROSS]


def relax_kernel(
    slabs,
    count_ref,
    cell_ref,
    weight_ref,
    volume_ref,
    velocity_ref,
    p_ref,
    solid_ref,
    d_ref,
    total_ref,
    va,
    vb,
    terms_ref,
    gathered,
    coef,
    a_ref,
    b_ref,
    x0,
    x1,
    y0,
    z0,
    rs_send,
    rs_recv,
    ag_send,
    ag_recv,
    halo_send,
    halo_recv,
    p_send,
    p_recv,
):
    quad = lax.axis_index("quad")
    slab = lax.axis_index("slab")
    nexts = lax.rem(slab + 1, slabs)
    prevs = lax.rem(slab + slabs - 1, slabs)
    peers = [lax.rem(quad + d, QUADS) for d in range(QUADS)]
    origins = [lax.rem(quad + QUADS - d, QUADS) for d in range(QUADS)]

    def at(q, s):
        return {"quad": q, "slab": s}

    def rows_of(q):
        return pl.ds(pl.multiple_of(q * CA, CA), CA)

    barrier = pltpu.get_barrier_semaphore()
    has_prev = slab > 0
    has_next = slab < slabs - 1

    def greet(where):
        pl.semaphore_signal(
            barrier, inc=1, device_id=where, device_id_type=pl.DeviceIdType.MESH
        )

    for d in range(1, QUADS):
        greet(at(peers[d], slab))

    @pl.when(has_next)
    def _():
        greet(at(quad, nexts))

    @pl.when(has_prev)
    def _():
        greet(at(quad, prevs))

    for buffer in (x0, x1, y0, z0, p_ref):
        rim = jnp.zeros((buffer.shape[0], 2, PAD, 128), F32)
        buffer[:, :, :PAD, :] = rim
        buffer[:, :, PAD + ACROSS :, :] = rim

    @pl.when(slab == 0)
    def _():
        for field in range(2):
            coef[field, 0:4] = jnp.zeros((4, 2, ACROSS, 128), F32)
        for buffer in (y0, z0):
            buffer[0:4] = jnp.zeros((4, 2, HELD, 128), F32)

    @pl.when(slab == slabs - 1)
    def _():
        for field in range(2):
            coef[field, 8:12] = jnp.zeros((4, 2, ACROSS, 128), F32)
        for buffer in (y0, z0):
            buffer[8:12] = jnp.zeros((4, 2, HELD, 128), F32)

    def link(src, dst, ssem, rsem, where):
        return pltpu.make_async_remote_copy(
            src_ref=src,
            dst_ref=dst,
            send_sem=ssem,
            recv_sem=rsem,
            device_id=where,
            device_id_type=pl.DeviceIdType.MESH,
        )

    def send(*args):
        copy = link(*args)
        copy.start()
        return copy

    def each_side(copies, up, down):
        @pl.when(has_next)
        def _():
            up(copies[0])

        @pl.when(has_prev)
        def _():
            down(copies[1])

    def start(copies):
        each_side(copies, lambda c: c.start(), lambda c: c.start())

    def sent(copies):
        each_side(copies, lambda c: c.wait_send(), lambda c: c.wait_send())

    def arrived(copies):
        each_side(copies[::-1], lambda c: c.wait_recv(), lambda c: c.wait_recv())

    scatter, gather, halos = [], [], []
    for f in range(2):
        deposit(f, count_ref, cell_ref, weight_ref, volume_ref, velocity_ref, d_ref, total_ref, va, vb)
        if f == 0:
            callers = QUADS - 1 + has_prev.astype(jnp.int32) + has_next.astype(jnp.int32)
            pl.semaphore_wait(barrier, callers)
        scatter.append(
            {
                d: send(
                    d_ref.at[f, :, :, rows_of(peers[d]), :],
                    gathered.at[f, d - 1],
                    rs_send.at[f, d - 1],
                    rs_recv.at[f, d - 1],
                    at(peers[d], slab),
                )
                for d in (2, 1, 3)
            }
        )
    own = rows_of(quad)

    def forward(f, d):
        block = rows_of(origins[d])
        src = coef.at[f, 4:8, :, block, :]
        pair = [
            link(
                src,
                coef.at[f, low : low + 4, :, block, :],
                halo_send.at[f, side, d],
                halo_recv.at[f, side, d],
                at(quad, where),
            )
            for side, (low, where) in enumerate(((0, nexts), (8, prevs)))
        ]
        start(pair)
        halos.append(pair)

    for f in range(2):
        for copy in scatter[f].values():
            copy.wait_recv()
        coef[f, 4:8, :, own, :] = (d_ref[f, :, :, own, :] + gathered[f, 0]) + (
            gathered[f, 1] + gathered[f, 2]
        )
        mine = coef.at[f, 4:8, :, own, :]
        gather.append(
            {
                d: send(mine, mine, ag_send.at[f, d - 1], ag_recv.at[f, d - 1], at(peers[d], slab))
                for d in (2, 1, 3)
            }
        )
        forward(f, 0)
    for f in range(2):
        for d in (1, 3, 2):
            gather[f][d].wait_recv()
            forward(f, d)

    for pair in halos:
        arrived(pair)


    lane = lax.broadcasted_iota(jnp.int32, (ACROSS, 128), 1)
    inner = slice(PAD, PAD + ACROSS)

    def coefficients(k, carry):
        inside = jnp.logical_and(
            jnp.logical_or(k >= 4, has_prev), jnp.logical_or(k <= 7, has_next)
        )
        thick = 1.0 + coef[0, k]
        ratio = jnp.where(inside, 1.0, 0.0) / (6.0 + 0.05 * thick)
        source = 4.0 * coef[1, k] * thick * ratio
        b_ref[k] = ratio
        a_ref[k] = source
        x0[k, :, inner, :] = source
        return carry

    lax.fori_loop(0, 12, coefficients, 0)
    def sweep(src, dst, begin, end, shift=0):
        half = (end - begin) // 2

        def body(i, carry):
            for j in range(half):
                k = begin + half * i + j
                for odd in range(2):
                    other = src[k, 1 - odd, inner, :]
                    if odd:
                        turned = jnp.where(lane < 127, pltpu.roll(other, 127, axis=1), 0.0)
                    else:
                        turned = jnp.where(lane > 0, pltpu.roll(other, 1, axis=1), 0.0)
                    total = src[k - 1, odd, inner, :] + src[k + 1, odd, inner, :]
                    total += src[k, odd, PAD - 1 : PAD + ACROSS - 1, :]
                    total += src[k, odd, PAD + 1 : PAD + ACROSS + 1, :]
                    total += other + turned
                    dst[k - shift, odd, inner, :] = a_ref[k, odd] + b_ref[k, odd] * total
            return carry

        lax.fori_loop(0, 2, body, 0)

    def exchange(buffer, n):
        def block(low):
            return buffer.at[low : low + 4, :, PAD : PAD + ACROSS, :]

        src = block(4)
        pair = [
            link(src, block(0), p_send.at[n, 0], p_recv.at[n, 0], at(quad, nexts)),
            link(src, block(8), p_send.at[n, 1], p_recv.at[n, 1], at(quad, prevs)),
        ]
        start(pair)
        return pair

    sweep(x0, x1, 1, 11)
    sweep(x1, x0, 2, 10)
    sweep(x0, x1, 3, 9)
    sweep(x1, y0, 4, 8)
    early = exchange(y0, 0)
    for pair in range(2):
        for odd in range(2):
            block = [coef[0, 4 + 2 * pair + j, odd] for j in range(2)]
            store_split(block, terms_ref, 0, 1, pair, odd)

    def keep(tile, sampled):
        solid_ref[:, tile] = sampled[0]

    sample(cell_ref, weight_ref, terms_ref, 1, keep)
    arrived(early)
    sweep(y0, x0, 1, 11)
    sweep(x0, x1, 2, 10)
    sweep(x1, x0, 3, 9)
    sweep(x0, z0, 4, 8)
    later = exchange(z0, 1)
    arrived(later)
    sweep(z0, x0, 1, 11)
    sweep(x0, x1, 2, 10)
    sweep(x1, p_ref, 3, 9, shift=3)

    for copies in scatter + gather:
        for copy in copies.values():
            copy.wait_send()
    for pair in halos + [early, later]:
        sent(pair)


def store_split(blocks, terms_ref, f, fields, pair, odd):
    hi, lo = split(jnp.concatenate(blocks, axis=0).T)
    r = f * CB + odd * HALF
    lanes = slice(pair * 128, (pair + 1) * 128)
    terms_ref[r : r + HALF, lanes] = hi
    terms_ref[r + fields * CB : r + fields * CB + HALF, lanes] = lo


def sample(cell_ref, weight_ref, terms_ref, fields, done):
    def one(base):
        tile = pl.ds(base, GTILE)
        rows = one_hot_rows(row_index(cell_ref[:, tile]), GTILE)
        weight = weight_ref[:, tile]
        upper = 1.0 - weight
        along, above = keys(cell_ref[:, tile])
        wanted = lax.broadcasted_iota(jnp.int32, (CB, GTILE), 0)
        pick = jnp.where(wanted == along, weight, jnp.where(wanted == above, upper, 0.0))
        both = jnp.dot(terms_ref[...], rows, preferred_element_type=F32)
        picked = both[: fields * CB] + both[fields * CB :]
        done(
            tile,
            [
                jnp.sum(pick * picked[f * CB : (f + 1) * CB], axis=0, keepdims=True)
                for f in range(fields)
            ],
        )

    def body(i, carry):
        for j in range(UNROLL):
            one(pl.multiple_of((i * UNROLL + j) * GTILE, GTILE))
        return carry

    lax.fori_loop(0, cell_ref.shape[1] // (GTILE * UNROLL), body, 0)


def sample_kernel(
    count_ref,
    cell_ref,
    weight_ref,
    volume_ref,
    velocity_ref,
    p_ref,
    solid_ref,
    pressure_ref,
    drag_ref,
    terms_ref,
    turned,
):
    lane = lax.broadcasted_iota(jnp.int32, (ACROSS, 128), 1)
    inner = slice(PAD, PAD + ACROSS)
    for pair in range(2):
        for odd in range(2):
            blocks = [[], [], []]
            for k in (2 * pair + 1, 2 * pair + 2):
                other = p_ref[k, 1 - odd, inner, :]
                if odd:
                    right, left = jnp.where(lane < 127, pltpu.roll(other, 127, axis=1), 0.0), other
                else:
                    right, left = other, jnp.where(lane > 0, pltpu.roll(other, 1, axis=1), 0.0)
                blocks[0].append(-0.5 * (p_ref[k + 1, odd, inner, :] - p_ref[k - 1, odd, inner, :]))
                blocks[1].append(
                    -0.5
                    * (
                        p_ref[k, odd, PAD + 1 : PAD + ACROSS + 1, :]
                        - p_ref[k, odd, PAD - 1 : PAD + ACROSS - 1, :]
                    )
                )
                blocks[2].append(-0.5 * (right - left))
            for f in range(3):
                store_split(blocks[f], terms_ref, f, 3, pair, odd)
    quad = lax.axis_index("quad")
    mine = pl.ds(pl.multiple_of(PAD + quad * CA, PAD), CA)
    swapped = jnp.concatenate(
        [p_ref[k + 1, odd, mine, :] for odd in range(2) for k in range(CH)], axis=0
    ).T
    turned[pl.ds(0, HALF, stride=2), :] = swapped
    turned[pl.ds(1, HALF, stride=2), :] = pltpu.roll(swapped, 64, axis=1)
    whole = turned[...].T
    for k in range(CH):
        pressure_ref[k] = whole[k * CA : (k + 1) * CA]

    def finish(tile, sampled):
        slots = tile.start + lax.broadcasted_iota(jnp.int32, (1, GTILE), 1)
        mass = jnp.where(slots < count_ref[0], volume_ref[:, tile], 0.0)
        factor = mass * (1.0 + solid_ref[:, tile]) ** 2
        for f in range(3):
            drag_ref[f : f + 1, tile] = factor * (sampled[f] - velocity_ref[f : f + 1, tile])

    sample(cell_ref, weight_ref, terms_ref, 3, finish)


def body(slabs, grain_cell, grain_count, grain_weight, grain_volume, grain_velocity):
    grains = grain_weight.shape[0]
    weight = grain_weight.reshape(1, grains)
    volume = grain_volume.reshape(1, grains)
    smem = pl.BlockSpec(memory_space=pltpu.SMEM)
    vmem = pl.BlockSpec(memory_space=pltpu.VMEM)
    dma = pltpu.SemaphoreType.DMA
    pressure, solid = pl.pallas_call(
        functools.partial(relax_kernel, slabs),
        out_shape=(
            jax.ShapeDtypeStruct((CH + 2, 2, HELD, 128), F32),
            jax.ShapeDtypeStruct((1, grains), F32),
        ),
        in_specs=[smem, vmem, vmem, vmem, vmem],
        out_specs=(vmem, vmem),
        scratch_shapes=[
            pltpu.VMEM((2, CH, 2, ACROSS, 128), F32),
            pltpu.VMEM((2 * CB, ROWS), F32),
            pltpu.VMEM((2 * CB, GBLOCK), BF16),
            pltpu.VMEM((2 * CB, GBLOCK), BF16),
            pltpu.VMEM((2 * CB, ROWS), BF16),
            pltpu.VMEM((2, 3, CH, 2, CA, 128), F32),
            pltpu.VMEM((2, 3 * CH, 2, ACROSS, 128), F32),
            pltpu.VMEM((3 * CH, 2, ACROSS, 128), F32),
            pltpu.VMEM((3 * CH, 2, ACROSS, 128), F32),
        ]
        + [pltpu.VMEM((3 * CH, 2, HELD, 128), F32)] * 4
        + [dma((2, 3))] * 4
        + [dma((2, 2, QUADS))] * 2
        + [dma((2, 2))] * 2,
        compiler_params=pltpu.CompilerParams(collective_id=0, has_side_effects=True),
        name="relax",
    )(grain_count, grain_cell, weight, volume, grain_velocity)
    return pl.pallas_call(
        sample_kernel,
        out_shape=(
            jax.ShapeDtypeStruct((CH, CA, CB), F32),
            jax.ShapeDtypeStruct((3, grains), F32),
        ),
        in_specs=[smem] + [vmem] * 6,
        out_specs=(vmem, vmem),
        scratch_shapes=[
            pltpu.VMEM((6 * CB, ROWS), BF16),
            pltpu.VMEM((CB, 128), F32),
        ],
        name="sample",
    )(grain_count, grain_cell, weight, volume, grain_velocity, pressure, solid)


def solution(mesh):
    placed = (
        P(None, ("slab", "quad")),
        P(("slab", "quad")),
        P(("slab", "quad")),
        P(("slab", "quad")),
        P(None, ("slab", "quad")),
    )
    return jax.shard_map(
        functools.partial(body, mesh.shape["slab"]),
        mesh=mesh,
        in_specs=placed,
        out_specs=(P("slab", "quad", None), P(None, ("slab", "quad"))),
        check_vma=False,
    )
```

time: 65 us -> 56.5 us (0.87)
  the two profiles are of different devices: /device:TPU:0 before, /device:TPU:121 now
where the time goes in v3:
time: 56.5 us; the launch traced here: 56.3 us
  Pallas kernels  55 us (97%)
  between operations  1.28 us (2%)
    pallas_call x1, Pallas kernels, body(): pl.pallas_call(functools.partial(relax_kernel, slabs), out_shape=(jax.Sha...  44.8 us
    pallas_call x1, Pallas kernels, body(): pl.pallas_call(sample_kernel, out_shape=(jax.ShapeDtypeStruct((CH, CA, CB...  10.3 us

profile of v3, /device:TPU:121, one launch (start us, length us, event | category | flops | bytes accessed | tf_op | source)
XLA Modules:
  0.0 56.3 jit_solution(2672667357111451803)
XLA Ops:
  1.3 44.8 %relax.1 = (f32[6,2,80,128]{3,2,1,0:T(8,128)}, f32[1,8192]{1,0:T(1,128)}) custom-call(s32[1]{0:T(128)S(6)} %copy.7.count_ref, s32[4,8192]{1,0:T(4,128)} %cell_ref.3, f32[1,8192]{1,0:T(1,128)} %bitcast.2, f32[1,8192]{1,0:T(1,128)} %bitcast.4, f32[3,8192]{1,0:T(4,128)} %velocity_ref.3), custom_call_target="tpu_custom_call" | custom-call | tf_op jit(solution)/shard_map/relax/pallas_call | solution.py:464
  46.1 10.3 %sample.1 = (f32[4,16,256]{2,1,0:T(8,128)}, f32[3,8192]{1,0:T(4,128)}) custom-call(s32[1]{0:T(128)S(6)} %copy.7.count_ref, s32[4,8192]{1,0:T(4,128)} %cell_ref.3, f32[1,8192]{1,0:T(1,128)} %bitcast.3, f32[1,8192]{1,0:T(1,128)} %bitcast.5, f32[3,8192]{1,0:T(4,128)} %velocity_ref.3, f32[6,2,80,128]{3,2,1,0:T(8,128)} %get-tuple-element.4.p_ref, ...), custom_call_target="tpu_custom_call" | custom-call | tf_op jit(solution)/shard_map/sample/pallas_call | solution.py:490

commit v4 on v3

--- a/solution.py
+++ b/solution.py
@@ -18,7 +18,7 @@
 HELD = ACROSS + 2 * PAD
 GBLOCK = 1024
 GTILE = 512
-UNROLL = 4
+UNROLL = 16
 
 F32 = jnp.float32
 BF16 = jnp.bfloat16
@@ -57,12 +57,11 @@
     return key(along), key(above)
 
 
-def deposit(field, count_ref, cell_ref, weight_ref, volume_ref, velocity_ref, out_ref, total, va, vb):
-    total[...] = jnp.zeros_like(total)
+def deposit(field, count_ref, cell_ref, weight_ref, volume_ref, velocity_ref, out_ref, total_ref, va, vb):
     blocks = cell_ref.shape[1] // GBLOCK
 
     def tile_of(t):
-        return pl.ds(pl.multiple_of(t * GBLOCK, GBLOCK), GBLOCK)
+        return slice(t * GBLOCK, (t + 1) * GBLOCK)
 
     def build(t, spread):
         tile = tile_of(t)
@@ -81,30 +80,32 @@
                     lower_hit, low, jnp.where(upper_hit, up, BF16(0.0))
                 )
 
-    def add(t, spread):
+    def product(t, spread):
         rows = one_hot_rows(row_index(cell_ref[:, tile_of(t)]), GBLOCK)
-        total[...] += lax.dot_general(
-            spread[...], rows, (((1,), (1,)), ((), ())), preferred_element_type=F32
-        )
-
+        return lax.dot_general(
+            rows, spread[...], (((1,), (1,)), ((), ())), preferred_element_type=F32
+        )
+
+    total = None
+    slots = (va, vb)
     build(0, va)
-
-    def body(i, carry):
-        t = 2 * i
-        build(t + 1, vb)
-        add(t, va)
-        build(jnp.minimum(t + 2, blocks - 1), va)
-        add(t + 1, vb)
+    for t in range(blocks):
+        if t + 1 < blocks:
+            build(t + 1, slots[(t + 1) % 2])
+        part = product(t, slots[t % 2])
+        total = part if total is None else total + part
+    total_ref[...] = total
+
+    def settle(layer, carry):
+        here = pl.ds(pl.multiple_of(layer * ACROSS, ACROSS), ACROSS)
+        for odd in range(2):
+            out_ref[field, layer, odd] = (
+                total_ref[here, odd * HALF : (odd + 1) * HALF]
+                + total_ref[here, CB + odd * HALF : CB + (odd + 1) * HALF]
+            )
         return carry
 
-    lax.fori_loop(0, blocks // 2, body, 0)
-    for pair in range(2):
-        lanes = slice(pair * 128, (pair + 1) * 128)
-        whole = total[:CB, lanes] + total[CB:, lanes]
-        for odd in range(2):
-            block = whole[odd * HALF : (odd + 1) * HALF].T
-            for j in range(2):
-                out_ref[field, 2 * pair + j, odd] = block[j * ACROSS : (j + 1) * ACROSS]
+    lax.fori_loop(0, CH, settle, 0)
 
 
 def relax_kernel(
@@ -171,25 +172,6 @@
     def _():
         greet(at(quad, prevs))
 
-    for buffer in (x0, x1, y0, z0, p_ref):
-        rim = jnp.zeros((buffer.shape[0], 2, PAD, 128), F32)
-        buffer[:, :, :PAD, :] = rim
-        buffer[:, :, PAD + ACROSS :, :] = rim
-
-    @pl.when(slab == 0)
-    def _():
-        for field in range(2):
-            coef[field, 0:4] = jnp.zeros((4, 2, ACROSS, 128), F32)
-        for buffer in (y0, z0):
-            buffer[0:4] = jnp.zeros((4, 2, HELD, 128), F32)
-
-    @pl.when(slab == slabs - 1)
-    def _():
-        for field in range(2):
-            coef[field, 8:12] = jnp.zeros((4, 2, ACROSS, 128), F32)
-        for buffer in (y0, z0):
-            buffer[8:12] = jnp.zeros((4, 2, HELD, 128), F32)
-
     def link(src, dst, ssem, rsem, where):
         return pltpu.make_async_remote_copy(
             src_ref=src,
@@ -241,6 +223,25 @@
                 for d in (2, 1, 3)
             }
         )
+    for buffer in (x0, x1, y0, z0, p_ref):
+        rim = jnp.zeros((buffer.shape[0], 2, PAD, 128), F32)
+        buffer[:, :, :PAD, :] = rim
+        buffer[:, :, PAD + ACROSS :, :] = rim
+
+    @pl.when(slab == 0)
+    def _():
+        for field in range(2):
+            coef[field, 0:4] = jnp.zeros((4, 2, ACROSS, 128), F32)
+        for buffer in (y0, z0):
+            buffer[0:4] = jnp.zeros((4, 2, HELD, 128), F32)
+
+    @pl.when(slab == slabs - 1)
+    def _():
+        for field in range(2):
+            coef[field, 8:12] = jnp.zeros((4, 2, ACROSS, 128), F32)
+        for buffer in (y0, z0):
+            buffer[8:12] = jnp.zeros((4, 2, HELD, 128), F32)
+
     own = rows_of(quad)
 
     def forward(f, d):
@@ -471,7 +472,7 @@
         out_specs=(vmem, vmem),
         scratch_shapes=[
             pltpu.VMEM((2, CH, 2, ACROSS, 128), F32),
-            pltpu.VMEM((2 * CB, ROWS), F32),
+            pltpu.VMEM((ROWS, 2 * CB), F32),
             pltpu.VMEM((2 * CB, GBLOCK), BF16),
             pltpu.VMEM((2 * CB, GBLOCK), BF16),
             pltpu.VMEM((2 * CB, ROWS), BF16),

time: 56.5 us -> 53.9 us (0.954)
  Pallas kernels: 55 us -> 52.5 us
    pallas_call x1, Pallas kernels: 44.8 us -> 43.3 us  [body(): pl.pallas_call(functools.partial(relax_kernel, slabs), out_shape=(jax.Sha...]
    pallas_call x1, Pallas kernels: 10.3 us -> 9.19 us  [body(): pl.pallas_call(sample_kernel, out_shape=(jax.ShapeDtypeStruct((CH, CA, CB...]
where the time goes in v4:
time: 53.9 us; the launch traced here: 53.8 us
  Pallas kernels  52.5 us (97%)
  between operations  1.28 us (2%)
    pallas_call x1, Pallas kernels, body(): pl.pallas_call(functools.partial(relax_kernel, slabs), out_shape=(jax.Sha...  43.3 us
    pallas_call x1, Pallas kernels, body(): pl.pallas_call(sample_kernel, out_shape=(jax.ShapeDtypeStruct((CH, CA, CB...  9.19 us

profile of v4, /device:TPU:121, one launch (start us, length us, event | category | flops | bytes accessed | tf_op | source)
XLA Modules:
  0.0 53.8 jit_solution(1797301896543047057)
XLA Ops:
  1.3 43.3 %relax.1 = (f32[6,2,80,128]{3,2,1,0:T(8,128)}, f32[1,8192]{1,0:T(1,128)}) custom-call(s32[1]{0:T(128)S(6)} %copy.7.count_ref, s32[4,8192]{1,0:T(4,128)} %cell_ref.3, f32[1,8192]{1,0:T(1,128)} %bitcast.2, f32[1,8192]{1,0:T(1,128)} %bitcast.4, f32[3,8192]{1,0:T(4,128)} %velocity_ref.3), custom_call_target="tpu_custom_call" | custom-call | tf_op jit(solution)/shard_map/relax/pallas_call | solution.py:465
  44.6 9.2 %sample.1 = (f32[4,16,256]{2,1,0:T(8,128)}, f32[3,8192]{1,0:T(4,128)}) custom-call(s32[1]{0:T(128)S(6)} %copy.7.count_ref, s32[4,8192]{1,0:T(4,128)} %cell_ref.3, f32[1,8192]{1,0:T(1,128)} %bitcast.3, f32[1,8192]{1,0:T(1,128)} %bitcast.5, f32[3,8192]{1,0:T(4,128)} %velocity_ref.3, f32[6,2,80,128]{3,2,1,0:T(8,128)} %get-tuple-element.4.p_ref, ...), custom_call_target="tpu_custom_call" | custom-call | tf_op jit(solution)/shard_map/sample/pallas_call | solution.py:491

commit v5 on v4

--- a/solution.py
+++ b/solution.py
@@ -44,7 +44,7 @@
 
 def masses(count_ref, vol, start, width):
     slots = start + lax.broadcasted_iota(jnp.int32, (1, width), 1)
-    return jnp.where(slots < count_ref[0], vol, 0.0)
+    return jnp.where(slots < count_ref[...], vol, 0.0)
 
 
 def keys(cell):
@@ -279,10 +279,6 @@
             gather[f][d].wait_recv()
             forward(f, d)
 
-    for pair in halos:
-        arrived(pair)
-
-
     lane = lax.broadcasted_iota(jnp.int32, (ACROSS, 128), 1)
     inner = slice(PAD, PAD + ACROSS)
 
@@ -298,7 +294,11 @@
         x0[k, :, inner, :] = source
         return carry
 
-    lax.fori_loop(0, 12, coefficients, 0)
+    lax.fori_loop(4, 8, coefficients, 0)
+    for pair in halos:
+        arrived(pair)
+    lax.fori_loop(0, 4, coefficients, 0)
+    lax.fori_loop(8, 12, coefficients, 0)
     def sweep(src, dst, begin, end, shift=0):
         half = (end - begin) // 2
 
@@ -447,7 +447,7 @@
 
     def finish(tile, sampled):
         slots = tile.start + lax.broadcasted_iota(jnp.int32, (1, GTILE), 1)
-        mass = jnp.where(slots < count_ref[0], volume_ref[:, tile], 0.0)
+        mass = jnp.where(slots < count_ref[...], volume_ref[:, tile], 0.0)
         factor = mass * (1.0 + solid_ref[:, tile]) ** 2
         for f in range(3):
             drag_ref[f : f + 1, tile] = factor * (sampled[f] - velocity_ref[f : f + 1, tile])
@@ -459,7 +459,7 @@
     grains = grain_weight.shape[0]
     weight = grain_weight.reshape(1, grains)
     volume = grain_volume.reshape(1, grains)
-    smem = pl.BlockSpec(memory_space=pltpu.SMEM)
+    count = grain_count.reshape(1, 1)
     vmem = pl.BlockSpec(memory_space=pltpu.VMEM)
     dma = pltpu.SemaphoreType.DMA
     pressure, solid = pl.pallas_call(
@@ -468,7 +468,7 @@
             jax.ShapeDtypeStruct((CH + 2, 2, HELD, 128), F32),
             jax.ShapeDtypeStruct((1, grains), F32),
         ),
-        in_specs=[smem, vmem, vmem, vmem, vmem],
+        in_specs=[vmem] * 5,
         out_specs=(vmem, vmem),
         scratch_shapes=[
             pltpu.VMEM((2, CH, 2, ACROSS, 128), F32),
@@ -487,21 +487,21 @@
         + [dma((2, 2))] * 2,
         compiler_params=pltpu.CompilerParams(collective_id=0, has_side_effects=True),
         name="relax",
-    )(grain_count, grain_cell, weight, volume, grain_velocity)
+    )(count, grain_cell, weight, volume, grain_velocity)
     return pl.pallas_call(
         sample_kernel,
         out_shape=(
             jax.ShapeDtypeStruct((CH, CA, CB), F32),
             jax.ShapeDtypeStruct((3, grains), F32),
         ),
-        in_specs=[smem] + [vmem] * 6,
+        in_specs=[vmem] * 7,
         out_specs=(vmem, vmem),
         scratch_shapes=[
             pltpu.VMEM((6 * CB, ROWS), BF16),
             pltpu.VMEM((CB, 128), F32),
         ],
         name="sample",
-    )(grain_count, grain_cell, weight, volume, grain_velocity, pressure, solid)
+    )(count, grain_cell, weight, volume, grain_velocity, pressure, solid)
 
 
 def solution(mesh):

time: 53.9 us -> 54.1 us (level)
  no operation moved by 1% of the time
where the time goes in v5:
time: 54.1 us; the launch traced here: 53.9 us
  Pallas kernels  52.6 us (97%)
  between operations  1.28 us (2%)
    pallas_call x1, Pallas kernels, body(): pl.pallas_call(functools.partial(relax_kernel, slabs), out_shape=(jax.Sha...  43.4 us
    pallas_call x1, Pallas kernels, body(): pl.pallas_call(sample_kernel, out_shape=(jax.ShapeDtypeStruct((CH, CA, CB...  9.23 us

profile of v5, /device:TPU:121, one launch (start us, length us, event | category | flops | bytes accessed | tf_op | source)
XLA Modules:
  0.0 53.9 jit_solution(15784908167258097260)
XLA Ops:
  1.3 43.4 %relax.1 = (f32[6,2,80,128]{3,2,1,0:T(8,128)}, f32[1,8192]{1,0:T(1,128)}) custom-call(s32[1,1]{1,0:T(1,128)} %bitcast.3.count_ref, s32[4,8192]{1,0:T(4,128)} %cell_ref.3, f32[1,8192]{1,0:T(1,128)} %bitcast.5, f32[1,8192]{1,0:T(1,128)} %bitcast.7, f32[3,8192]{1,0:T(4,128)} %velocity_ref.3), custom_call_target="tpu_custom_call" | custom-call | tf_op jit(solution)/shard_map/relax/pallas_call | solution.py:465
  44.7 9.2 %sample.1 = (f32[4,16,256]{2,1,0:T(8,128)}, f32[3,8192]{1,0:T(4,128)}) custom-call(s32[1,1]{1,0:T(1,128)} %bitcast.4.count_ref, s32[4,8192]{1,0:T(4,128)} %cell_ref.3, f32[1,8192]{1,0:T(1,128)} %bitcast.6, f32[1,8192]{1,0:T(1,128)} %bitcast.8, f32[3,8192]{1,0:T(4,128)} %velocity_ref.3, f32[6,2,80,128]{3,2,1,0:T(8,128)} %get-tuple-element.4.p_ref, ...), custom_call_target="tpu_custom_call" | custom-call | tf_op jit(solution)/shard_map/sample/pallas_call | solution.py:491
